TPU v7x, 32 devices: a whole 2x2x4 slice. The times are simulated.
32 devices in a mesh: replica: 8 (over y, x, core), shard: 4 (over z).
Axes of the slice: x: 2, y: 2, z: 4, core: 2. Of those that a mesh axis runs over, the one named last changes fastest.
Arguments:
- tokens: bfloat16 [8192, 1536], P(('replica', 'shard')), may hold values from -8 to 8
- cotangent: bfloat16 [8192, 1536], P(('replica', 'shard')), may hold values from -6 to 6
- attn_gain: bfloat16 [1536], P('shard'), may hold values from 0.5 to 1.5
- w_query: bfloat16 [1536, 1536], P('shard'), may hold values from -0.17860863 to 0.17860863
- w_key: bfloat16 [1536, 768], P('shard'), may hold values from -0.17860863 to 0.17860863
- w_value: bfloat16 [1536, 768], P('shard'), may hold values from -0.15625 to 0.15625
- w_out: bfloat16 [1536, 1536], P('shard'), may hold values from -0.625 to 0.625
- mlp_gain: bfloat16 [1536], P('shard'), may hold values from 0.5 to 1.5
- w_gate: bfloat16 [1536, 4096], P('shard'), may hold values from -0.15625 to 0.15625
- w_up: bfloat16 [1536, 4096], P('shard'), may hold values from -0.15625 to 0.15625
- w_down: bfloat16 [4096, 1536], P('shard'), may hold values from -0.09375 to 0.09375
Outputs:
- block_output: bfloat16 [8192, 1536], P(('replica', 'shard'))
- input_grad: float32 [8192, 1536], P(('replica', 'shard'))
- attn_gain_grad: float32 [1536], P('shard')
- query_grad: float32 [1536, 1536], P('shard')
- key_grad: float32 [1536, 768], P('shard')
- value_grad: float32 [1536, 768], P('shard')
- out_grad: float32 [1536, 1536], P('shard')
- mlp_gain_grad: float32 [1536], P('shard')
- gate_grad: float32 [1536, 4096], P('shard')
- up_grad: float32 [1536, 4096], P('shard')
- down_grad: float32 [4096, 1536], P('shard')
All inputs are finite; a program needn't handle non-finite values.
Results may differ from a plain program's by a relative error of at most 0.014.
Values may be sent and summed in bfloat16 or wider, within the bound.
No kernel may reach another device: no remote copies, remote signals or barrier semaphores. Data moves between devices by JAX's collectives and lax.ppermute only.
A program may use at most 384 MiB of HBM per device.

v0:
```python
import functools
import math

import jax
import jax.numpy as jnp
from jax import lax
from jax.experimental import pallas as pl
from jax.experimental.pallas import tpu as pltpu
from jax.sharding import PartitionSpec as P


HEAD_DIM = 96
LANES = 128
NORM_EPS = 1e-05
ROPE_BASE = 100000.0
VMEM_BYTES = 60 * 1024 * 1024
MLP_VMEM_BYTES = 40 * 1024 * 1024
F32 = jnp.float32
BF16 = jnp.bfloat16


def nn(left, right):
    return jnp.dot(left, right, preferred_element_type=F32)


def nt(left, right):
    return lax.dot_general(left, right, (((1,), (1,)), ((), ())), preferred_element_type=F32)


def tn(left, right):
    return lax.dot_general(left, right, (((0,), (0,)), ((), ())), preferred_element_type=F32)


def swap(x, bit):
    size = lax.axis_size("replica")
    return lax.ppermute(x, "replica", [(i, i ^ bit) for i in range(size)])


def plane_gather(x, high):
    cut = x.shape[0] // 2
    got = {0: (x,)}
    if len(high) == 2:
        a, b = high
        from_a, from_b = swap(x, a), swap(x, b)
        got[a], got[b] = (from_a,), (from_b,)
        got[1] = (swap(x, 1),)
        far = swap(from_b[:cut], a), swap(from_a[cut:], b)
        got[a ^ b] = far
    else:
        for bit in high:
            more = {j ^ bit: tuple(swap(p, bit) for p in got[j]) for j in list(got)}
            got.update(more)
    for j in list(got):
        if j ^ 1 not in got:
            got[j ^ 1] = tuple(swap(p, 1) for p in got[j])
    return got


def plane_scatter(parts, high):
    cut = parts[0].shape[0] // 2
    even = [j for j in parts if j % 2 == 0]
    both = {j: (parts[j], swap(parts[j ^ 1], 1)) for j in even}

    def total(terms, rows):
        return sum(t[rows].astype(F32) for t in terms).astype(BF16)

    low, top, full = slice(0, cut), slice(cut, 2 * cut), slice(0, 2 * cut)
    if len(high) == 2:
        a, b = high
        far, near_a, near_b = both[a ^ b], both[a], both[b]
        via_a = swap(total(far, low), a)
        via_b = swap(total(far, top), b)
        first_a = swap(total(near_a, low), a)
        first_b = swap(total(near_b, top), b)
        last_a = (total32(near_a, top) + via_b.astype(F32)).astype(BF16)
        last_b = (total32(near_b, low) + via_a.astype(F32)).astype(BF16)
        last_a, last_b = swap(last_a, a), swap(last_b, b)
        return both[0], (first_a, last_b), (last_a, first_b)
    sums = {j: total(both[j], full) for j in even}
    for bit in reversed(high):
        sums = {j: total((sums[j], swap(sums[j ^ bit], bit)), full) for j in sums if not j & bit}
    return (sums[0],), (), ()


def total32(terms, rows):
    return sum(t[rows].astype(F32) for t in terms)


def flat(terms):
    return [y for group in terms for y in group]


def call(kernel, inputs, outputs, scratch=(), flops=0, exps=0, limit=VMEM_BYTES):
    outputs = [jax.ShapeDtypeStruct(shape, kind) for shape, kind in outputs]
    moved = sum(math.prod(y.shape) * y.dtype.itemsize for y in [*inputs, *outputs])
    return pl.pallas_call(
        kernel,
        out_shape=outputs,
        scratch_shapes=list(scratch),
        compiler_params=pltpu.CompilerParams(vmem_limit_bytes=limit),
        cost_estimate=pl.CostEstimate(flops=flops, bytes_accessed=moved, transcendentals=exps),
    )(*inputs)


def rope_tables(length):
    half = HEAD_DIM // 2
    position = jnp.arange(length, dtype=F32)
    freqs = jnp.power(ROPE_BASE, -jnp.arange(half, dtype=F32) / half)
    angles = position[:, None] * freqs[None, :]
    pad = ((0, 0), (0, LANES // 2 - half))
    cosine, sine = jnp.pad(jnp.cos(angles), pad), jnp.pad(jnp.sin(angles), pad)
    return jnp.concatenate([cosine, cosine], 1), jnp.concatenate([-sine, sine], 1)


def turn(values, cosine, sine):
    return values * cosine + pltpu.roll(values, LANES // 2, 1) * sine


def turn_back(values, cosine, sine):
    return values * cosine - pltpu.roll(values, LANES // 2, 1) * sine


def head_probs(query, key):
    length = query.shape[0]
    scores = nt(query, key) * HEAD_DIM ** (-0.5)
    rows = lax.broadcasted_iota(jnp.int32, (length, length), 0)
    columns = lax.broadcasted_iota(jnp.int32, (length, length), 1)
    scores = jnp.where(rows >= columns, scores, -jnp.inf)
    raised = jnp.exp(scores - jnp.max(scores, -1, keepdims=True))
    return raised / jnp.sum(raised, -1, keepdims=True)


def head_span(k):
    return slice(k * LANES, (k + 1) * LANES)


def load(refs):
    parts = [r[...] for r in refs]
    return parts[0] if len(parts) == 1 else jnp.concatenate(parts, 0)


def take(refs, counts):
    refs, out = list(refs), []
    for count in counts:
        out.append(refs[:count])
        refs = refs[count:]
    return out, refs


def inverse_rms(rows):
    return lax.rsqrt(jnp.mean(rows * rows, -1, keepdims=True) + NORM_EPS)


def attn_forward_kernel(queries, keys, counts, *refs):
    blocks, rest = take(refs, counts)
    gain_ref, w_ref, wo_ref, pick_ref, cos_ref, sin_ref = rest[:6]
    parts, (h_ref, qkv_ref, o_ref) = rest[6 : 6 + len(blocks)], rest[6 + len(blocks) :]
    cosine, sine = cos_ref[...], sin_ref[...]
    length = cosine.shape[0]
    for n, block in enumerate(blocks):
        at_rows = slice(n * length, (n + 1) * length)
        x = load(block).astype(F32)
        normed = (x * inverse_rms(x) * gain_ref[...]).astype(BF16)
        h_ref[at_rows, :] = normed
        mixed = nn(normed, w_ref[...])
        made = []
        for k in range(queries + 2 * keys):
            piece = mixed[:, head_span(k)]
            made.append((turn(piece, cosine, sine) if k < queries + keys else piece).astype(BF16))
            qkv_ref[at_rows, head_span(k)] = made[k]
        heads = []
        for k in range(queries):
            at = k * keys // queries
            probs = head_probs(made[k], made[queries + at])
            heads.append(nn(probs.astype(BF16), made[queries + keys + at]).astype(BF16))
        heads = nn(jnp.concatenate(heads, 1), pick_ref[...]).astype(BF16)
        o_ref[at_rows, :] = heads
        parts[n][...] = nn(heads, wo_ref[...]).astype(BF16)


def attn_forward(blocks, gain, w, wo, pick, tables, queries, keys):
    counts = [len(b) for b in blocks]
    length, width = tables[0].shape[0], w.shape[0]
    rows = length * len(blocks)
    *parts, h, qkv, o = call(
        functools.partial(attn_forward_kernel, queries, keys, counts),
        [*flat(blocks), gain, w, wo, pick, *tables],
        [((length, width), BF16)] * len(blocks)
        + [((rows, width), BF16), ((rows, w.shape[1]), BF16), ((rows, wo.shape[0]), BF16)],
        flops=2 * rows * width * (w.shape[1] + wo.shape[0]) + 4 * rows * length * queries * LANES,
        exps=rows * length * queries,
    )
    return parts, (h, qkv, o)


def mlp_kernel(counts, *refs):
    blocks, rest = take(refs, counts)
    half = len(blocks) // 2
    wgu_ref, wd_ref = rest[:2]
    outs, dhs = rest[2 : 2 + half], rest[2 + half : 2 + 2 * half]
    dgu_ref, at_ref, h_ref, c_ref, a_ref = rest[2 + 2 * half :]
    length = outs[0].shape[0]
    for n in range(half):
        h_ref[n * length : (n + 1) * length, :] = load(blocks[n])
        c_ref[n * length : (n + 1) * length, :] = load(blocks[half + n])
    hidden, width = wd_ref.shape
    tile = min(hidden, 2 * LANES)

    def first(k, carry):
        at = pl.multiple_of(k * tile, tile)
        over = pl.multiple_of(hidden + k * tile, tile)
        gate = nn(h_ref[...], wgu_ref[:, pl.ds(at, tile)])
        upward = nn(h_ref[...], wgu_ref[:, pl.ds(over, tile)])
        d_active = nt(c_ref[...], wd_ref[pl.ds(at, tile), :])
        sigmoid = jax.nn.sigmoid(gate)
        silu = gate * sigmoid
        active = (silu * upward).astype(BF16)
        a_ref[:, pl.ds(at, tile)] = active
        at_ref[pl.ds(at, tile), :] = active.T
        d_gate = d_active * upward * sigmoid * (1.0 + gate * (1.0 - sigmoid))
        dgu_ref[:, pl.ds(at, tile)] = d_gate.astype(BF16)
        dgu_ref[:, pl.ds(over, tile)] = (d_active * silu).astype(BF16)
        return carry

    lax.fori_loop(0, hidden // tile, first, 0)
    wtile = 2 * LANES

    def second(k, carry):
        at = pl.ds(pl.multiple_of(k * wtile, wtile), wtile)
        d_normed = nt(dgu_ref[...], wgu_ref[at, :]).astype(BF16)
        output = nn(a_ref[...], wd_ref[:, at]).astype(BF16)
        for n in range(half):
            dhs[n][:, at] = d_normed[n * length : (n + 1) * length]
            outs[n][:, at] = output[n * length : (n + 1) * length]
        return carry

    lax.fori_loop(0, width // wtile, second, 0)


def mlp_both(h, c, wgu, wd):
    counts = [len(b) for b in [*h, *c]]
    half = len(h)
    length, width, hidden = sum(p.shape[0] for p in h[0]), wgu.shape[0], wd.shape[0]
    rows = half * length
    made = call(
        functools.partial(mlp_kernel, counts),
        [*flat(h), *flat(c), wgu, wd],
        [((length, width), BF16)] * (2 * half)
        + [((rows, 2 * hidden), BF16), ((hidden, rows), BF16)],
        scratch=[
            pltpu.VMEM((rows, width), BF16),
            pltpu.VMEM((rows, width), BF16),
            pltpu.VMEM((rows, hidden), BF16),
        ],
        flops=12 * rows * width * hidden,
        exps=rows * hidden,
        limit=MLP_VMEM_BYTES,
    )
    return made[:half], made[half : 2 * half], made[2 * half], made[2 * half + 1]


def stack_rows(parts, out):
    at = 0
    for part in parts:
        out[at : at + part.shape[0], :] = part[...]
        at += part.shape[0]


def wide_grads_kernel(count, pieces, *refs):
    hs, ds, (g_ref, h_all, d_all) = refs[:pieces], refs[pieces : pieces + count], refs[pieces + count :]

    @pl.when(pl.program_id(0) == 0)
    def _():
        stack_rows(ds, d_all)

    stack_rows(hs, h_all)
    g_ref[...] = tn(h_all[...], d_all[...]).astype(BF16)


def down_grads_kernel(count, pieces, *refs):
    ats, cs, (g_ref, at_all, c_all) = refs[:count], refs[count : count + pieces], refs[count + pieces :]

    @pl.when(pl.program_id(0) == 0)
    def _():
        at = 0
        for across in ats:
            at_all[:, at : at + across.shape[1]] = across[...]
            at += across.shape[1]

    stack_rows(cs, c_all)
    g_ref[...] = nn(at_all[...], c_all[...]).astype(BF16)


def attn_backward_kernel(queries, keys, counts, *refs):
    blocks, rest = take(refs, counts)
    qkv_ref, w_ref, wo_ref, pick_ref, cos_ref, sin_ref = rest[:6]
    dhs, (dqkv_ref,) = rest[6 : 6 + len(blocks)], rest[6 + len(blocks) :]
    cosine, sine = cos_ref[...], sin_ref[...]
    length = cosine.shape[0]
    each = queries // keys
    scale = HEAD_DIM ** (-0.5)
    for n, block in enumerate(blocks):
        at_rows = slice(n * length, (n + 1) * length)
        d_heads = nt(load(block), wo_ref[...]).astype(BF16)
        d_heads = nt(d_heads, pick_ref[...]).astype(BF16)
        for at in range(keys):
            key = qkv_ref[at_rows, head_span(queries + at)]
            value = qkv_ref[at_rows, head_span(queries + keys + at)]
            d_key, d_value = 0.0, 0.0
            for k in range(at * each, (at + 1) * each):
                query = qkv_ref[at_rows, head_span(k)]
                d_head = d_heads[:, head_span(k)]
                probs = head_probs(query, key)
                d_value += tn(probs.astype(BF16), d_head)
                d_probs = nt(d_head, value)
                delta = jnp.sum(probs * d_probs, -1, keepdims=True)
                d_scores = (probs * (d_probs - delta) * scale).astype(BF16)
                d_query = nn(d_scores, key)
                d_key += tn(d_scores, query)
                dqkv_ref[at_rows, head_span(k)] = turn_back(d_query, cosine, sine).astype(BF16)
            dqkv_ref[at_rows, head_span(queries + at)] = turn_back(d_key, cosine, sine).astype(BF16)
            dqkv_ref[at_rows, head_span(queries + keys + at)] = d_value.astype(BF16)
    wtile = 2 * LANES

    def second(k, carry):
        at = pl.ds(pl.multiple_of(k * wtile, wtile), wtile)
        d_normed = nt(dqkv_ref[...], w_ref[at, :]).astype(BF16)
        for n in range(len(blocks)):
            dhs[n][:, at] = d_normed[n * length : (n + 1) * length]
        return carry

    lax.fori_loop(0, w_ref.shape[0] // wtile, second, 0)


def attn_backward(blocks, qkv, w, wo, pick, tables, queries, keys):
    counts = [len(b) for b in blocks]
    length, width = tables[0].shape[0], w.shape[0]
    rows = length * len(blocks)
    *dhs, dqkv = call(
        functools.partial(attn_backward_kernel, queries, keys, counts),
        [*flat(blocks), qkv, w, wo, pick, *tables],
        [((length, width), BF16)] * len(blocks) + [((rows, w.shape[1]), BF16)],
        flops=2 * rows * width * (w.shape[1] + wo.shape[0]) + 10 * rows * length * queries * LANES,
        exps=rows * length * queries,
    )
    return dhs, dqkv


def attn_grads_kernel(count, *refs):
    hs, ds, pick_ref = refs[:count], refs[count : 2 * count], refs[2 * count]
    g_ref, h_all, d_all = refs[2 * count + 1 :]

    @pl.when(pl.program_id(0) == 0)
    def _():
        stack_rows(ds, d_all)

    stack_rows(hs, h_all)
    grad = tn(h_all[...], d_all[...]).astype(BF16)
    g_ref[...] = nt(grad, pick_ref[...]).astype(BF16)


def out_grads_kernel(count, pieces, *refs):
    os, ms, (g_ref, o_all, m_all) = refs[:count], refs[count : count + pieces], refs[count + pieces :]

    @pl.when(pl.program_id(0) == 0)
    def _():
        stack_rows(os, o_all)

    stack_rows(ms, m_all)
    g_ref[...] = tn(o_all[...], m_all[...]).astype(BF16)


def grads_call(kernel, tiled, fixed, consts, out, along, flops, held=None):
    tile = 2 * LANES
    rows, width = sum(y.shape[0] for y in tiled), tiled[0].shape[1]
    held = held or (rows, fixed[0].shape[1])
    whole = lambda y: pl.BlockSpec(y.shape, lambda i: (0, 0), pipeline_mode=pl.Buffered(1))
    part = lambda y: pl.BlockSpec((y.shape[0], tile), lambda i: (0, i))
    moving, resident = pltpu.VMEM((rows, tile), BF16), pltpu.VMEM(held, BF16)
    if along == 0:
        inputs = [*tiled, *fixed, *consts]
        specs = [part(y) for y in tiled] + [whole(y) for y in [*fixed, *consts]]
        out_spec = pl.BlockSpec((tile, out[1]), lambda i: (i, 0))
        scratch = [moving, resident]
    else:
        inputs, specs = [*fixed, *tiled], [whole(y) for y in fixed] + [part(y) for y in tiled]
        out_spec = pl.BlockSpec((out[0], tile), lambda i: (0, i))
        scratch = [resident, moving]
    return pl.pallas_call(
        kernel,
        grid=(width // tile,),
        in_specs=specs,
        out_specs=out_spec,
        out_shape=jax.ShapeDtypeStruct(out, BF16),
        scratch_shapes=scratch,
        compiler_params=pltpu.CompilerParams(
            dimension_semantics=("arbitrary",), vmem_limit_bytes=VMEM_BYTES
        ),
        cost_estimate=pl.CostEstimate(flops=flops, bytes_accessed=3 * rows * width, transcendentals=0),
    )(*inputs)


def finish_kernel(kind, counts, *refs):
    (whole, low, top), rest = take(refs, counts)
    length = whole[0].shape[0]
    cut = length // 2
    halves = []
    for half, extra in ((0, low), (1, top)):
        rows = slice(half * cut, (half + 1) * cut)
        total = sum(t[rows, :].astype(F32) for t in whole)
        halves.append(sum((t[...].astype(F32) for t in extra), total))
    total = jnp.concatenate(halves, 0)
    if kind == "middle":
        x_ref, gain_ref, middle_ref, h_ref = rest
        middle = x_ref[...].astype(F32) + total
        middle_ref[...] = middle
        h_ref[...] = (middle * inverse_rms(middle) * gain_ref[...]).astype(BF16)
    elif kind == "output":
        middle_ref, out_ref = rest
        out_ref[...] = (middle_ref[...] + total).astype(BF16)
    else:
        rows_ref, base_ref, gain_ref, *outs = rest
        rows = rows_ref[...].astype(F32)
        inverse = inverse_rms(rows)
        scaled = total * gain_ref[...]
        mean = jnp.mean(scaled * rows, -1, keepdims=True)
        made = base_ref[...].astype(F32) + inverse * scaled - rows * inverse**3 * mean
        for out in outs:
            out[...] = made.astype(out.dtype)


def finish(kind, terms, extras, kinds):
    counts = [len(t) for t in terms]
    shape = terms[0][0].shape
    return call(
        functools.partial(finish_kernel, kind, counts),
        [*flat(terms), *extras],
        [(shape, k) for k in kinds],
        flops=16 * math.prod(shape),
    )


def spread_kernel(at_ref, gate_ref, up_ref, down_ref, wg_ref, wu_ref, gate_out, up_out, down_out, gain_out):
    gate, upward = gate_ref[0].astype(F32), up_ref[0].astype(F32)
    gate_out[...] = gate
    up_out[...] = upward
    down_out[...] = down_ref[0].astype(F32)

    @pl.when((pl.program_id(0) == 0) & (pl.program_id(1) == 0))
    def _():
        gain_out[...] = jnp.zeros_like(gain_out)

    gain_out[...] += gate * wg_ref[...].astype(F32) + upward * wu_ref[...].astype(F32)


def spread(at, gate_up, down, w_gate, w_up, parts):
    count, width, wide = gate_up.shape
    tile = wide // 2 // parts
    short = down.shape[1] // parts
    columns = pl.BlockSpec((width, tile), lambda a, s, at: (0, s * count + a))
    spec = pltpu.PrefetchScalarGridSpec(
        num_scalar_prefetch=1,
        grid=(count, parts),
        in_specs=[
            pl.BlockSpec((1, width, tile), lambda a, s, at: (a ^ at[0], 0, s)),
            pl.BlockSpec((1, width, tile), lambda a, s, at: (a ^ at[0], 0, parts + s)),
            pl.BlockSpec((1, short, down.shape[2]), lambda a, s, at: (a ^ at[0], s, 0)),
            columns,
            columns,
        ],
        out_specs=[
            columns,
            columns,
            pl.BlockSpec((short, down.shape[2]), lambda a, s, at: (a * parts + s, 0)),
            pl.BlockSpec((width, tile), lambda a, s, at: (0, 0)),
        ],
    )
    return pl.pallas_call(
        spread_kernel,
        grid_spec=spec,
        out_shape=[
            jax.ShapeDtypeStruct((width, count * wide // 2), F32),
            jax.ShapeDtypeStruct((width, count * wide // 2), F32),
            jax.ShapeDtypeStruct((count * down.shape[1], down.shape[2]), F32),
            jax.ShapeDtypeStruct((width, tile), F32),
        ],
        compiler_params=pltpu.CompilerParams(dimension_semantics=("arbitrary", "arbitrary")),
        cost_estimate=pl.CostEstimate(
            flops=0, bytes_accessed=6 * (gate_up.size + down.size), transcendentals=0
        ),
        name="spread",
    )(at, gate_up, gate_up, down, w_gate, w_up)


def spread_attn_kernel(count, cuts, at_ref, *refs):
    blocks, (wq_ref, wk_ref, wv_ref), (q_out, k_out, v_out, gain_out) = refs[:count], refs[count : count + 3], refs[count + 3 :]

    @pl.when(pl.program_id(0) == 0)
    def _():
        gain_out[...] = jnp.zeros_like(gain_out)

    total = 0.0
    spans = ((0, cuts[0]), (cuts[0], cuts[1]), (cuts[1], blocks[0].shape[2]))
    for (low, high), out, w_ref in zip(spans, (q_out, k_out, v_out), (wq_ref, wk_ref, wv_ref)):
        made = jnp.concatenate([b[0, :, low:high].astype(F32) for b in blocks], 1)
        out[...] = made
        total += jnp.sum(made * w_ref[...].astype(F32), 1, keepdims=True)
    gain_out[...] += total


def spread_attn(at, stack, weights, cuts):
    group, slab, narrow = stack.shape
    count = LANES // math.gcd(LANES, HEAD_DIM)
    count = math.gcd(group, count)
    widths = (cuts[0], cuts[1] - cuts[0], narrow - cuts[1])
    columns = [pl.BlockSpec((slab, count * w), lambda p, at: (0, p)) for w in widths]

    def block(i):
        return pl.BlockSpec((1, slab, narrow), lambda p, at: ((p * count + i) ^ at[0], 0, 0))

    return pl.pallas_call(
        functools.partial(spread_attn_kernel, count, cuts),
        grid_spec=pltpu.PrefetchScalarGridSpec(
            num_scalar_prefetch=1,
            grid=(group // count,),
            in_specs=[block(i) for i in range(count)] + columns,
            out_specs=columns + [pl.BlockSpec((slab, 1), lambda p, at: (0, 0))],
        ),
        out_shape=[jax.ShapeDtypeStruct((slab, group * w), F32) for w in widths]
        + [jax.ShapeDtypeStruct((slab, 1), F32)],
        compiler_params=pltpu.CompilerParams(dimension_semantics=("arbitrary",)),
        cost_estimate=pl.CostEstimate(flops=0, bytes_accessed=8 * stack.size, transcendentals=0),
        name="spread_attn",
    )(at, *[stack] * count, *weights)


def head_columns(queries, keys):
    half, lane = HEAD_DIM // 2, jnp.arange(LANES)
    place = lane % (LANES // 2)
    turned = jnp.where(place < half, (lane // (LANES // 2)) * half + place, -1)
    plain = jnp.where(lane < HEAD_DIM, lane, -1)
    columns = []
    for k in range(queries + 2 * keys):
        inside = turned if k < queries + keys else plain
        columns.append(jnp.where(inside >= 0, inside + k * HEAD_DIM, -1))
    return jnp.concatenate(columns)


def gather_shard(x):
    return lax.all_gather(x, "shard", axis=0, tiled=True)


def scatter_shard(x):
    return lax.psum_scatter(x, "shard", scatter_dimension=0, tiled=True)


def after(x, *others):
    return lax.optimization_barrier((x, *others))[0]


def layer(
    tokens, cotangent, attn_gain, w_query, w_key, w_value, w_out, mlp_gain, w_gate, w_up, w_down
):
    replicas, shards = lax.axis_size("replica"), lax.axis_size("shard")
    length, width = tokens.shape
    slab = w_query.shape[0]
    kv_heads = w_key.shape[1] // HEAD_DIM
    group = math.gcd(replicas, kv_heads)
    keys = kv_heads // group
    queries = w_query.shape[1] // HEAD_DIM // group
    high = [1 << k for k in range(1, group.bit_length() - 1)]
    place = lax.axis_index("replica") % group
    hidden = w_down.shape[0] // group
    narrow = (queries + 2 * keys) * HEAD_DIM

    x = plane_gather(tokens, high)

    wq = lax.dynamic_slice_in_dim(w_query, place * queries * HEAD_DIM, queries * HEAD_DIM, 1)
    wk = lax.dynamic_slice_in_dim(w_key, place * keys * HEAD_DIM, keys * HEAD_DIM, 1)
    wv = lax.dynamic_slice_in_dim(w_value, place * keys * HEAD_DIM, keys * HEAD_DIM, 1)
    spare = 16
    gain_rows = -(-slab // narrow)
    gains = jnp.stack([attn_gain, mlp_gain])
    gains = jnp.pad(gains, ((0, 0), (0, gain_rows * narrow - slab))).reshape(2 * gain_rows, narrow)
    gains = jnp.pad(gains, ((0, spare - 2 * gain_rows), (0, 0)))
    sent = jnp.concatenate([jnp.concatenate([wq, wk, wv], 1), gains], 0)
    both = gather_shard(sent).reshape(shards, slab + spare, narrow)
    w_out, w_gate_s, w_up_s, w_down_s, _ = lax.optimization_barrier((w_out, w_gate, w_up, w_down, sent))

    turns = group // shards
    chunk = w_out.shape[0] // group
    mine = lax.dynamic_slice_in_dim(w_out, place * chunk, chunk, 0)
    routes = []
    for turn_by in range(shards):
        route = []
        for i in range(replicas):
            base, q = i - i % group, i % group
            for z in range(shards):
                to = (base + z * turns + q // shards) * shards + (q + turn_by) % shards
                route.append((i * shards + z, to))
        routes.append(route)
    back = [(b, a) for a, b in routes[0]]
    came = []
    for route in routes:
        came.append(lax.ppermute(mine, ("replica", "shard"), route))
    here = lax.axis_index("shard")
    came = jnp.stack(came)[(here - jnp.arange(shards)) % shards]
    wo = came.reshape(shards * chunk, width)

    columns = head_columns(queries, keys)
    pick = (jnp.arange(narrow)[:, None] == columns[None, :]).astype(BF16)
    wqkv = nn(both[:, :slab].reshape(width, narrow), pick).astype(BF16)
    gains = both[:, slab : slab + 2 * gain_rows].reshape(shards, 2, gain_rows * narrow)[:, :, :slab]
    gains = jnp.moveaxis(gains, 1, 0).reshape(2, 1, width).astype(F32)
    gain_a, gain_m = gains[0], gains[1]
    lanes = jnp.arange(queries * LANES)
    heads = (lanes // LANES) * HEAD_DIM + lanes % LANES
    heads = jnp.where(lanes % LANES < HEAD_DIM, heads, -1)
    pick_o = (jnp.arange(queries * HEAD_DIM)[None, :] == heads[:, None]).astype(BF16)

    wgu = jnp.concatenate(
        [
            lax.dynamic_slice_in_dim(w, s * group * hidden + place * hidden, hidden, 1)
            for w in (w_gate_s, w_up_s)
            for s in range(shards)
        ],
        1,
    )
    wd = lax.dynamic_slice_in_dim(w_down_s, place * hidden, hidden, 0)
    wgu = gather_shard(wgu)
    wd = gather_shard(wd)

    c = plane_gather(after(cotangent, *x[high[0]], *x[high[-1]]), high)

    pairs = [j for j in sorted(x, reverse=True) if j % 2 == 0]
    tables = rope_tables(length)
    parts, saved = {}, {}
    for j in pairs:
        (parts[j ^ 1], parts[j]), saved[j] = attn_forward(
            [x[j ^ 1], x[j]], gain_a, wqkv, wo, pick_o, tables, queries, keys
        )
    middle, h_own = finish("middle", plane_scatter(parts, high), [tokens, gain_m], [F32, BF16])
    h = plane_gather(h_own, high)

    order = list(reversed(pairs))
    order = order[:-2] + [order[-1], order[-2]] if len(order) > 2 else order
    outs, dhs, dgus, acrosses = {}, {}, [], []
    for j in order:
        (outs[j ^ 1], outs[j]), (dhs[j ^ 1], dhs[j]), dgu, across = mlp_both(
            [h[j ^ 1], h[j]], [c[j ^ 1], c[j]], wgu, wd
        )
        dgus.append(dgu)
        acrosses.append(across)
    d_middle, dm_own = finish(
        "back", plane_scatter(dhs, high), [middle, cotangent, gain_m], [F32, BF16]
    )
    all_h = flat(h[k] for j in order for k in (j ^ 1, j))
    all_c = flat(c[k] for j in order for k in (j ^ 1, j))
    rows = group * length
    g_gu = grads_call(
        functools.partial(wide_grads_kernel, len(dgus), len(all_h)),
        all_h, dgus, [], wgu.shape, 0, 2 * rows * width * wgu.shape[1],
    )
    g_d = grads_call(
        functools.partial(down_grads_kernel, len(acrosses), len(all_c)),
        all_c, acrosses, [], wd.shape, 1, 2 * rows * width * wd.shape[0],
        (wd.shape[0], rows),
    )
    g_gu, g_d = scatter_shard(g_gu), scatter_shard(g_d)
    dm = plane_gather(dm_own, high)
    all_dm = flat(dm[k] for j in order for k in (j ^ 1, j))
    g_o = grads_call(
        functools.partial(out_grads_kernel, len(pairs), len(all_dm)),
        all_dm, [saved[j][2] for j in order], [], wo.shape, 1,
        2 * rows * width * wo.shape[0],
    )
    g_o = lax.ppermute(scatter_shard(g_o), ("replica", "shard"), back)

    das, dqkvs = {}, []
    for j in order:
        (das[j ^ 1], das[j]), dqkv = attn_backward(
            [dm[j ^ 1], dm[j]], saved[j][1], wqkv, wo, pick_o, tables, queries, keys
        )
        dqkvs.append(dqkv)
    g_w = grads_call(
        functools.partial(attn_grads_kernel, len(pairs)),
        [saved[j][0] for j in order], dqkvs, [pick], (width, narrow), 0,
        2 * rows * width * pick.shape[1],
    )
    g_w = scatter_shard(g_w)
    (input_grad,) = finish("back", plane_scatter(das, high), [tokens, d_middle, gain_a], [F32])

    outs = dict(zip(outs, (after(y, *all_dm) for y in outs.values())))
    (block_output,) = finish("output", plane_scatter(outs, high), [middle], [BF16])

    bit = group
    while bit < replicas:
        g_gu, g_d, g_w, g_o = (g + swap(g, bit) for g in (g_gu, g_d, g_w, g_o))
        bit *= 2

    def stacked(g):
        got = plane_gather(g, high)
        return jnp.concatenate(flat(got[j] for j in range(group)), 0).reshape(group, *g.shape)

    gate_grad, up_grad, down_grad, gain_terms = spread(
        place.reshape(1), stacked(g_gu), stacked(g_d), w_gate, w_up, shards
    )
    mlp_gain_grad = jnp.sum(gain_terms, 1) / mlp_gain.astype(F32)
    absolute = jnp.arange(group) ^ place
    out_grad = stacked(g_o)[absolute].astype(F32).reshape(group * chunk, width)
    cuts = (queries * HEAD_DIM, (queries + keys) * HEAD_DIM)
    query_grad, key_grad, value_grad, gain_terms = spread_attn(
        place.reshape(1), stacked(g_w), (w_query, w_key, w_value), cuts
    )
    attn_gain_grad = gain_terms[:, 0] / attn_gain.astype(F32)
    return (
        block_output,
        input_grad,
        attn_gain_grad,
        query_grad,
        key_grad,
        value_grad,
        out_grad,
        mlp_gain_grad,
        gate_grad,
        up_grad,
        down_grad,
    )


def solution(mesh):
    tokens, weights, gains = P(("replica", "shard"), None), P("shard", None), P("shard")
    return jax.shard_map(
        layer,
        mesh=mesh,
        in_specs=(tokens, tokens, gains, weights, weights, weights, weights, gains, weights, weights, weights),
        out_specs=(tokens, tokens, gains, weights, weights, weights, weights, gains, weights, weights, weights),
        check_vma=False,
    )
```

profile of v0, /device:TPU:0, one launch (start us, length us, event | category | flops | bytes accessed | tf_op | source)
XLA Modules:
  0.0 625.8 jit_solution(15668231643220527656)
XLA Ops:
  13.9 7.0 %collective-permute-start.4 = (bf16[48,1536]{1,0:T(8,128)(2,1)S(1)}, bf16[48,1536]{1,0:T(8,128)(2,1)S(1)}, u32[]{:S(2)}, u32[]{:S(2)}) collective-permute-start(bf16[48,1536]{1,0:T(8,128)(2,1)S(1)} %constant_dynamic-slice_fusion.1), channel_id=1, source_target_pairs={{0,3},{1,11},{2,19},{3,27},{4,0},{5,8},{6,16},{7,24},{8,1},{9,9},{... | collective-permute-start | bytes 442376 | tf_op jit(solution)/shard_map/ppermute | solution.py:605
  37.8 9.0 %collective-permute-done.10.refs_1_ = bf16[256,1536]{1,0:T(8,128)(2,1)} collective-permute-done((bf16[256,1536]{1,0:T(8,128)(2,1)}, bf16[256,1536]{1,0:T(8,128)(2,1)}, u32[]{:S(2)}, u32[]{:S(2)}) %collective-permute-start.10) | collective-permute-done | bytes 786464 | tf_op jit(solution)/shard_map/ppermute | solution.py:36
  48.8 3.8 collective-permute-start.13
  56.9 7.3 %collective-permute-done.13.refs_2_ = bf16[128,1536]{1,0:T(8,128)(2,1)} collective-permute-done((bf16[128,1536]{1,0:T(8,128)(2,1)S(1)}, bf16[128,1536]{1,0:T(8,128)(2,1)}, u32[]{:S(2)}, u32[]{:S(2)}) %collective-permute-start.13) | collective-permute-done | bytes 393248 | tf_op jit(solution)/shard_map/ppermute | solution.py:36
  70.4 6.9 %shard_map.197 = (bf16[256,1536]{1,0:T(8,128)(2,1)}, bf16[256,1536]{1,0:T(8,128)(2,1)}, bf16[512,1536]{1,0:T(8,128)(2,1)}, bf16[512,512]{1,0:T(8,128)(2,1)}, bf16[512,192]{1,0:T(8,128)(2,1)}) custom-call(bf16[128,1536]{1,0:T(8,128)(2,1)} %copy-done.94, bf16[128,1536]{1,0:T(8,128)(2,1)} %collective-permute-done.16.refs_1_, ...), custom_call_target="tpu_custom_call" | custom-call | flops 1241513984 | bytes 7968768 | tf_op jit(solution)/shard_map/pallas_call | solution.py:96
  77.9 7.0 %shard_map.195 = (bf16[256,1536]{1,0:T(8,128)(2,1)}, bf16[256,1536]{1,0:T(8,128)(2,1)}, bf16[512,1536]{1,0:T(8,128)(2,1)}, bf16[512,512]{1,0:T(8,128)(2,1)}, bf16[512,192]{1,0:T(8,128)(2,1)}) custom-call(bf16[256,1536]{1,0:T(8,128)(2,1)} %collective-permute-done.7.refs_0_, bf16[256,1536]{1,0:T(8,128)(2,1)} %copy-done.85, f32[1,1536]{1,0:T(1,128)} %bitcast.52, ...), custom_call_target="tpu_custom_call" | custom-call | flops 1241513984 | bytes 7968768 | tf_op jit(solution)/shard_map/pallas_call | solution.py:96
  89.4 6.9 %shard_map.196 = (bf16[256,1536]{1,0:T(8,128)(2,1)}, bf16[256,1536]{1,0:T(8,128)(2,1)}, bf16[512,1536]{1,0:T(8,128)(2,1)}, bf16[512,512]{1,0:T(8,128)(2,1)}, bf16[512,192]{1,0:T(8,128)(2,1)}) custom-call(bf16[256,1536]{1,0:T(8,128)(2,1)} %copy-done.93, bf16[256,1536]{1,0:T(8,128)(2,1)} %collective-permute-done.10.refs_1_, f32[1,1536]{1,0:T(1,128)} %bitcast.53, ...), custom_call_target="tpu_custom_call" | custom-call | flops 1241513984 | bytes 7968768 | tf_op jit(solution)/shard_map/pallas_call | solution.py:96
  96.5 7.4 %shard_map.194 = (bf16[256,1536]{1,0:T(8,128)(2,1)}, bf16[256,1536]{1,0:T(8,128)(2,1)}, bf16[512,1536]{1,0:T(8,128)(2,1)}, bf16[512,512]{1,0:T(8,128)(2,1)}, bf16[512,192]{1,0:T(8,128)(2,1)}) custom-call(bf16[256,1536]{1,0:T(8,128)(2,1)} %collective-permute-done.refs_0_, bf16[256,1536]{1,0:T(8,128)(2,1)} %refs_6_.4, f32[1,1536]{1,0:T(1,128)} %bitcast.54, ...), custom_call_target="tpu_custom_call" | custom-call | flops 1241513984 | bytes 7968768 | tf_op jit(solution)/shard_map/pallas_call | solution.py:96
  108.4 8.0 %collective-permute-done.18 = bf16[128,1536]{1,0:T(8,128)(2,1)S(1)} collective-permute-done((bf16[128,1536]{1,0:T(8,128)(2,1)}, bf16[128,1536]{1,0:T(8,128)(2,1)S(1)}, u32[]{:S(2)}, u32[]{:S(2)}) %collective-permute-start.18) | collective-permute-done | bytes 393248 | tf_op jit(solution)/shard_map/ppermute | solution.py:36
  128.7 4.6 collective-permute-done.21.refs_4_
  133.2 3.9 collective-permute-done.22.refs_5_
  137.9 4.1 shard_map.198
  144.4 9.7 %collective-permute-done.34.refs_3_.refs_13_ = bf16[256,1536]{1,0:T(8,128)(2,1)} collective-permute-done((bf16[256,1536]{1,0:T(8,128)(2,1)S(1)}, bf16[256,1536]{1,0:T(8,128)(2,1)}, u32[]{:S(2)}, u32[]{:S(2)}) %collective-permute-start.34) | collective-permute-done | bytes 786464 | tf_op jit(solution)/shard_map/ppermute | solution.py:36
  157.7 13.2 %collective-permute-done.32.refs_1_.refs_9_ = bf16[256,1536]{1,0:T(8,128)(2,1)} collective-permute-done((bf16[256,1536]{1,0:T(8,128)(2,1)}, bf16[256,1536]{1,0:T(8,128)(2,1)}, u32[]{:S(2)}, u32[]{:S(2)}) %collective-permute-start.32) | collective-permute-done | bytes 786464 | tf_op jit(solution)/shard_map/ppermute | solution.py:36
  201.0 6.9 %shard_map.202 = (bf16[256,1536]{1,0:T(8,128)(2,1)S(1)}, bf16[256,1536]{1,0:T(8,128)(2,1)S(1)}, bf16[256,1536]{1,0:T(8,128)(2,1)S(1)}, bf16[256,1536]{1,0:T(8,12...) custom-call(bf16[128,1536]{1,0:T(8,128)(2,1)S(1)} %copy-done.25, ...), custom_call_target="tpu_custom_call" | custom-call | flops 4831838208 | bytes 12582912 | tf_op jit(solution)/shard_map/pallas_call | solution.py:96
  211.2 8.5 %shard_map.199 = (bf16[256,1536]{1,0:T(8,128)(2,1)S(1)}, bf16[256,1536]{1,0:T(8,128)(2,1)S(1)}, bf16[256,1536]{1,0:T(8,128)(2,1)S(1)}, bf16[256,1536]{1,0:T(8,12...) custom-call(bf16[256,1536]{1,0:T(8,128)(2,1)} %collective-permute-done.23.refs_0_, ...), custom_call_target="tpu_custom_call" | custom-call | flops 4831838208 | bytes 12582912 | tf_op jit(solution)/shard_map/pallas_call | solution.py:96
  222.5 9.8 %shard_map.200 = (bf16[256,1536]{1,0:T(8,128)(2,1)S(1)}, bf16[256,1536]{1,0:T(8,128)(2,1)S(1)}, bf16[256,1536]{1,0:T(8,128)(2,1)}, bf16[256,1536]{1,0:T(8,128)(2...) custom-call(bf16[256,1536]{1,0:T(8,128)(2,1)} %collective-permute-done.27.refs_0_.refs_2_, ...), custom_call_target="tpu_custom_call" | custom-call | flops 4831838208 | bytes 12582912 | tf_op jit(solution)/shard_map/pallas_call | solution.py:96
  234.8 9.9 %shard_map.201 = (bf16[256,1536]{1,0:T(8,128)(2,1)}, bf16[256,1536]{1,0:T(8,128)(2,1)S(1)}, bf16[256,1536]{1,0:T(8,128)(2,1)}, bf16[256,1536]{1,0:T(8,128)(2,1)S...) custom-call(bf16[256,1536]{1,0:T(8,128)(2,1)S(1)} %collective-permute-done.33.refs_0_.refs_8_, ...), custom_call_target="tpu_custom_call" | custom-call | flops 4831838208 | bytes 12582912 | tf_op jit(solution)/shard_map/pallas_call | solution.py:96
  247.4 8.7 %shard_map.213 = bf16[512,1536]{1,0:T(8,128)(2,1)} custom-call(bf16[512,512]{1,0:T(8,128)(2,1)} %copy-done.37, bf16[512,512]{1,0:T(8,128)(2,1)} %copy-done.38, bf16[512,512]{1,0:T(8,128)(2,1)} %copy-done.36, bf16[512,512]{1,0:T(8,128)(2,1)} %copy-done.39, bf16[256,1536]{1,0:T(8,128)(2,1)} %collective-permute-done.24.refs_2_.refs_4_, ...), custom_call_target="tpu_custom_call" | custom-call | flops 3221225472 | bytes 9437184 | tf_op jit(solution)/shard_map/pallas_call | solution.py:389
  260.4 8.6 %collective-permute-done.46 = bf16[128,1536]{1,0:T(8,128)(2,1)S(1)} collective-permute-done((bf16[128,1536]{1,0:T(8,128)(2,1)}, bf16[128,1536]{1,0:T(8,128)(2,1)S(1)}, u32[]{:S(2)}, u32[]{:S(2)}) %collective-permute-start.46) | collective-permute-done | bytes 393248 | tf_op jit(solution)/shard_map/ppermute | solution.py:36
  277.5 5.0 collective-permute-done.47.refs_3_
  288.5 5.5 shard_map.203
  296.5 14.7 %collective-permute-done.54.refs_1_.refs_13_ = bf16[256,1536]{1,0:T(8,128)(2,1)S(1)} collective-permute-done((bf16[256,1536]{1,0:T(8,128)(2,1)}, bf16[256,1536]{1,0:T(8,128)(2,1)S(1)}, u32[]{:S(2)}, u32[]{:S(2)}) %collective-permute-start.54) | collective-permute-done | bytes 786464 | tf_op jit(solution)/shard_map/ppermute | solution.py:36
  314.5 6.1 collective-permute-done.55.refs_2_.refs_10_
  320.6 4.8 collective-permute-done.57.refs_3_.refs_11_
  328.3 7.5 %shard_map.211 = bf16[192,1536]{1,0:T(8,128)(2,1)} custom-call(bf16[512,192]{1,0:T(8,128)(2,1)} %get-tuple-element.157.refs_0_, bf16[512,192]{1,0:T(8,128)(2,1)} %get-tuple-element.158.refs_1_, bf16[512,192]{1,0:T(8,128)(2,1)} %get-tuple-element.159.refs_2_, bf16[512,192]{1,0:T(8,128)(2,1)} %get-tuple-element.160.refs_3_, bf16[256,1536]{1,0:T(8,128)(2,1)} %copy-done.62, ...), custom_call_target="tpu_custom_call" | custom-call | flops 1207959552 | bytes 9437184 | tf_op jit(solution)/shard_map/pallas_call | solution.py:389
  336.7 9.5 %shard_map.205 = (bf16[256,1536]{1,0:T(8,128)(2,1)}, bf16[256,1536]{1,0:T(8,128)(2,1)}, bf16[512,512]{1,0:T(8,128)(2,1)}) custom-call(bf16[256,1536]{1,0:T(8,128)(2,1)} %copy-done.62, bf16[256,1536]{1,0:T(8,128)(2,1)} %get-tuple-element.116.refs_1_.refs_5_, bf16[512,512]{1,0:T(8,128)(2,1)} %get-tuple-element.132.refs_2_, ...), custom_call_target="tpu_custom_call" | custom-call | flops 1442840576 | bytes 6717440 | tf_op jit(solution)/shard_map/pallas_call | solution.py:96
  346.2 9.5 %shard_map.208 = (bf16[256,1536]{1,0:T(8,128)(2,1)}, bf16[256,1536]{1,0:T(8,128)(2,1)}, bf16[512,512]{1,0:T(8,128)(2,1)}) custom-call(bf16[128,1536]{1,0:T(8,128)(2,1)} %copy-done.81, bf16[128,1536]{1,0:T(8,128)(2,1)} %copy-done.82, bf16[128,1536]{1,0:T(8,128)(2,1)} %copy-done.78, bf16[128,1536]{1,0:T(8,128)(2,1)} %copy-done.79, ...), custom_call_target="tpu_custom_call" | custom-call | flops 1442840576 | bytes 6717440 | tf_op jit(solution)/shard_map/pallas_call | solution.py:96
  355.7 9.5 %shard_map.206 = (bf16[256,1536]{1,0:T(8,128)(2,1)}, bf16[256,1536]{1,0:T(8,128)(2,1)}, bf16[512,512]{1,0:T(8,128)(2,1)}) custom-call(bf16[256,1536]{1,0:T(8,128)(2,1)} %copy-done.61, bf16[256,1536]{1,0:T(8,128)(2,1)} %copy-done.48, bf16[512,512]{1,0:T(8,128)(2,1)} %get-tuple-element.135.refs_2_, bf16[1536,512]{1,0:T(8,128)(2,1)} %convolution_convert_fusion.refs_3_.refs_5_, ...), custom_call_target="tpu_custom_call" | custom-call | flops 1442840576 | bytes 6717440 | tf_op jit(solution)/shard_map/pallas_call | solution.py:96
  365.1 9.5 %shard_map.207 = (bf16[256,1536]{1,0:T(8,128)(2,1)}, bf16[256,1536]{1,0:T(8,128)(2,1)}, bf16[512,512]{1,0:T(8,128)(2,1)}) custom-call(bf16[256,1536]{1,0:T(8,128)(2,1)} %copy-done.60, bf16[256,1536]{1,0:T(8,128)(2,1)} %copy-done.47, bf16[512,512]{1,0:T(8,128)(2,1)} %get-tuple-element.138.refs_2_, bf16[1536,512]{1,0:T(8,128)(2,1)} %convolution_convert_fusion.refs_3_.refs_5_, ...), custom_call_target="tpu_custom_call" | custom-call | flops 1442840576 | bytes 6717440 | tf_op jit(solution)/shard_map/pallas_call | solution.py:96
  374.6 9.4 %shard_map.210 = bf16[1536,384]{1,0:T(8,128)(2,1)} custom-call(bf16[512,1536]{1,0:T(8,128)(2,1)} %get-tuple-element.145.refs_0_, bf16[512,1536]{1,0:T(8,128)(2,1)} %get-tuple-element.146.refs_1_, bf16[512,1536]{1,0:T(8,128)(2,1)} %get-tuple-element.147.refs_2_, bf16[512,1536]{1,0:T(8,128)(2,1)} %get-tuple-element.148.refs_3_, ...), custom_call_target="tpu_custom_call" | custom-call | flops 3221225472 | bytes 9437184 | tf_op jit(solution)/shard_map/pallas_call | solution.py:389
  386.1 12.2 %shard_map.212 = bf16[1536,1024]{1,0:T(8,128)(2,1)} custom-call(bf16[256,1536]{1,0:T(8,128)(2,1)} %collective-permute-done.23.refs_0_, bf16[256,1536]{1,0:T(8,128)(2,1)} %get-tuple-element.101.refs_1_, bf16[256,1536]{1,0:T(8,128)(2,1)} %collective-permute-done.27.refs_0_.refs_2_, bf16[256,1536]{1,0:T(8,128)(2,1)} %copy-done.7, bf16[128,1536]{1,0:T(8,128)(2,1)} %copy-done.24, ...), custom_call_target="tpu_custom_call" | custom-call | flops 6442450944 | bytes 9437184 | tf_op jit(solution)/shard_map/pallas_call | solution.py:389
  407.2 6.5 %collective-permute-done.113 = bf16[64,1536]{1,0:T(8,128)(2,1)S(1)} collective-permute-done((bf16[64,1536]{1,0:T(8,128)(2,1)S(1)}, bf16[64,1536]{1,0:T(8,128)(2,1)S(1)}, u32[]{:S(2)}, u32[]{:S(2)}) %collective-permute-start.113) | collective-permute-done | bytes 196640 | tf_op jit(solution)/shard_map/ppermute | solution.py:36
  415.0 4.9 collective-permute-done.114
  430.2 7.1 %collective-permute-done.67 = bf16[128,1536]{1,0:T(8,128)(2,1)} collective-permute-done((bf16[128,1536]{1,0:T(8,128)(2,1)S(1)}, bf16[128,1536]{1,0:T(8,128)(2,1)}, u32[]{:S(2)}, u32[]{:S(2)}) %collective-permute-start.67) | collective-permute-done | bytes 393248 | tf_op jit(solution)/shard_map/ppermute | solution.py:36
  444.0 5.1 collective-permute-start.93
  453.8 10.6 %collective-permute-start.75 = (bf16[128,1536]{1,0:T(8,128)(2,1)}, bf16[128,1536]{1,0:T(8,128)(2,1)S(1)}, u32[]{:S(2)}, u32[]{:S(2)}) collective-permute-start(bf16[128,1536]{1,0:T(8,128)(2,1)} %get-tuple-element.178), channel_id=1, source_target_pairs={{0,8},{4,12},{8,0},{12,4},{16,24},{20,28},{24,16},{28,20},{1,9},{5... | collective-permute-start | bytes 1179656 | tf_op jit(solution)/shard_map/ppermute | solution.py:36
  472.4 5.8 collective-permute-start.90
  481.4 12.5 %collective-permute-done.95 = bf16[24,1536]{1,0:T(8,128)(2,1)S(1)} collective-permute-done((bf16[24,1536]{1,0:T(8,128)(2,1)S(1)}, bf16[24,1536]{1,0:T(8,128)(2,1)S(1)}, u32[]{:S(2)}, u32[]{:S(2)}) %collective-permute-start.95) | collective-permute-done | bytes 73760 | tf_op jit(solution)/shard_map/ppermute | solution.py:36
  493.9 4.3 collective-permute-done.96
  506.4 3.7 shard_map.204
  513.9 5.4 collective-permute-done.78.refs_4_
  522.2 5.1 shard_map.209
  531.5 7.3 %collective-permute-done.81 = bf16[384,384]{1,0:T(8,128)(2,1)} collective-permute-done((bf16[384,384]{1,0:T(8,128)(2,1)}, bf16[384,384]{1,0:T(8,128)(2,1)}, u32[]{:S(2)}, u32[]{:S(2)}) %collective-permute-start.81) | collective-permute-done | bytes 294944 | tf_op jit(solution)/shard_map/ppermute | solution.py:36
  552.8 11.2 %collective-permute-done.100 = bf16[384,1024]{1,0:T(8,128)(2,1)S(1)} collective-permute-done((bf16[384,1024]{1,0:T(8,128)(2,1)}, bf16[384,1024]{1,0:T(8,128)(2,1)S(1)}, u32[]{:S(2)}, u32[]{:S(2)}) %collective-permute-start.100) | collective-permute-done | bytes 786464 | tf_op jit(solution)/shard_map/ppermute | solution.py:36
  565.4 4.9 spread_attn.1
  581.0 3.7 collective-permute-done.104
  593.6 23.4 %spread.1 = (f32[384,4096]{1,0:T(8,128)}, f32[384,4096]{1,0:T(8,128)}, f32[1024,1536]{1,0:T(8,128)}, f32[384,128]{1,0:T(8,128)}) custom-call(s32[1]{0:T(128)} %bitcast.9.at_ref, bf16[8,384,1024]{2,1,0:T(8,128)(2,1)} %bitcast.14.gate_ref.up_ref, bf16[8,384,1024]{2,1,0:T(8,128)(2,1)} %bitcast.14.gate_ref.up_ref, bf16[8,128,1536]{2,1,0:T(8,128)(2,1)} %bitcast.32, ...), custom_call_target="tpu_custom_call" | custom-call | bytes 28311552 | tf_op jit(solution)/shard_map/spread/pallas_call | solution.py:478
  (533 shorter events, 234.4 us)
Async XLA Ops:
  7.2 57.5 %all-gather.4.cloned.1.call-start = ((), (), s32[]{:S(2)}) async-start(), calls=%async_computation.4 | async-start | bytes 1536000 | tf_op jit(solution)/shard_map/all_gather | solution.py:550
  12.0 178.8 %all-gather.8.cloned.1.call-start = ((), (), s32[]{:S(2)}) async-start(), calls=%async_computation.6 | async-start | bytes 1966080 | tf_op jit(solution)/shard_map/all_gather | solution.py:550
  12.9 177.9 %all-gather.6.cloned.1.call-start = ((), (), s32[]{:S(2)}) async-start(), calls=%async_computation.5 | async-start | bytes 3932160 | tf_op jit(solution)/shard_map/all_gather | solution.py:550
  13.9 38.7 %collective-permute-start.4 = (bf16[48,1536]{1,0:T(8,128)(2,1)S(1)}, bf16[48,1536]{1,0:T(8,128)(2,1)S(1)}, u32[]{:S(2)}, u32[]{:S(2)}) collective-permute-start(bf16[48,1536]{1,0:T(8,128)(2,1)S(1)} %constant_dynamic-slice_fusion.1), channel_id=1, source_target_pairs={{0,3},{1,11},{2,19},{3,27},{4,0},{5,8},{6,16},{7,24},{8,1},{9,9},{... | collective-permute-start | bytes 442376 | tf_op jit(solution)/shard_map/ppermute | solution.py:605
  20.9 34.5 %collective-permute-start.3 = (bf16[48,1536]{1,0:T(8,128)(2,1)S(1)}, bf16[48,1536]{1,0:T(8,128)(2,1)S(1)}, u32[]{:S(2)}, u32[]{:S(2)}) collective-permute-start(bf16[48,1536]{1,0:T(8,128)(2,1)S(1)} %constant_dynamic-slice_fusion.1), channel_id=1, source_target_pairs={{0,2},{1,10},{2,18},{3,26},{4,3},{5,11},{6,19},{7,27},{8,0},{9,8},... | collective-permute-start | bytes 442376 | tf_op jit(solution)/shard_map/ppermute | solution.py:605
  22.5 32.9 %collective-permute-start.2 = (bf16[48,1536]{1,0:T(8,128)(2,1)S(1)}, bf16[48,1536]{1,0:T(8,128)(2,1)S(1)}, u32[]{:S(2)}, u32[]{:S(2)}) collective-permute-start(bf16[48,1536]{1,0:T(8,128)(2,1)S(1)} %constant_dynamic-slice_fusion.1), channel_id=1, source_target_pairs={{0,1},{1,9},{2,17},{3,25},{4,2},{5,10},{6,18},{7,26},{8,3},{9,11},... | collective-permute-start | bytes 442376 | tf_op jit(solution)/shard_map/ppermute | solution.py:605
  24.7 22.1 %collective-permute-start.10 = (bf16[256,1536]{1,0:T(8,128)(2,1)}, bf16[256,1536]{1,0:T(8,128)(2,1)}, u32[]{:S(2)}, u32[]{:S(2)}) collective-permute-start(bf16[256,1536]{1,0:T(8,128)(2,1)} %refs_6_.4), channel_id=1, source_target_pairs={{0,16},{4,20},{8,24},{12,28},{16,0},{20,4},{24,8},{28,12},{1,17},{... | collective-permute-start | bytes 2359304 | tf_op jit(solution)/shard_map/ppermute | solution.py:36
  26.9 22.0 %collective-permute-start.6 = (bf16[256,1536]{1,0:T(8,128)(2,1)}, bf16[256,1536]{1,0:T(8,128)(2,1)S(1)}, u32[]{:S(2)}, u32[]{:S(2)}) collective-permute-start(bf16[256,1536]{1,0:T(8,128)(2,1)} %refs_6_.4), channel_id=1, source_target_pairs={{0,8},{4,12},{8,0},{12,4},{16,24},{20,28},{24,16},{28,20},{1,9},{5... | collective-permute-start | bytes 2359304 | tf_op jit(solution)/shard_map/ppermute | solution.py:36
  36.4 347.8 %reduce-scatter.11.cloned.1.call-start = ((), (), s32[]{:S(2)}) async-start(), calls=%async_computation.10 | async-start | bytes 1966080 | tf_op jit(solution)/shard_map/reduce_scatter | solution.py:554
  56.9 21.0 %collective-permute-start.7 = (bf16[256,1536]{1,0:T(8,128)(2,1)S(1)}, bf16[256,1536]{1,0:T(8,128)(2,1)}, u32[]{:S(2)}, u32[]{:S(2)}) collective-permute-start(bf16[256,1536]{1,0:T(8,128)(2,1)S(1)} %collective-permute-done.6.refs_1_), channel_id=1, source_target_pairs={{0,4},{4,0},{8,12},{12,8},{16,20},{20,16},{24,28},{28,24},{1,5},{5... | collective-permute-start | bytes 2359304 | tf_op jit(solution)/shard_map/ppermute | solution.py:36
  77.8 18.7 %collective-permute-start = (bf16[256,1536]{1,0:T(8,128)(2,1)S(1)}, bf16[256,1536]{1,0:T(8,128)(2,1)}, u32[]{:S(2)}, u32[]{:S(2)}) collective-permute-start(bf16[256,1536]{1,0:T(8,128)(2,1)S(1)} %copy-done.46), channel_id=1, source_target_pairs={{0,4},{4,0},{8,12},{12,8},{16,20},{20,16},{24,28},{28,24},{1,5},{5... | collective-permute-start | bytes 2359304 | tf_op jit(solution)/shard_map/ppermute | solution.py:36
  84.8 20.9 %collective-permute-start.8 = (bf16[256,1536]{1,0:T(8,128)(2,1)}, bf16[256,1536]{1,0:T(8,128)(2,1)S(1)}, u32[]{:S(2)}, u32[]{:S(2)}) collective-permute-start(bf16[256,1536]{1,0:T(8,128)(2,1)} %get-tuple-element.96), channel_id=1, source_target_pairs={{0,4},{4,0},{8,12},{12,8},{16,20},{20,16},{24,28},{28,24},{1,5},{5... | collective-permute-start | bytes 2359304 | tf_op jit(solution)/shard_map/ppermute | solution.py:36
  86.3 19.4 %collective-permute-start.20 = (bf16[128,1536]{1,0:T(8,128)(2,1)}, bf16[128,1536]{1,0:T(8,128)(2,1)S(1)}, u32[]{:S(2)}, u32[]{:S(2)}) collective-permute-start(bf16[128,1536]{1,0:T(8,128)(2,1)} %get-tuple-element.195), channel_id=1, source_target_pairs={{0,16},{4,20},{8,24},{12,28},{16,0},{20,4},{24,8},{28,12},{1,17},{... | collective-permute-start | bytes 1179656 | tf_op jit(solution)/shard_map/ppermute | solution.py:36
  120.3 33.8 %collective-permute-start.34 = (bf16[256,1536]{1,0:T(8,128)(2,1)S(1)}, bf16[256,1536]{1,0:T(8,128)(2,1)}, u32[]{:S(2)}, u32[]{:S(2)}) collective-permute-start(bf16[256,1536]{1,0:T(8,128)(2,1)S(1)} %copy-done.4), channel_id=1, source_target_pairs={{0,16},{4,20},{8,24},{12,28},{16,0},{20,4},{24,8},{28,12},{1,17},{... | collective-permute-start | bytes 2359304 | tf_op jit(solution)/shard_map/ppermute | solution.py:36
  124.8 31.9 %collective-permute-start.28 = (bf16[256,1536]{1,0:T(8,128)(2,1)S(1)}, bf16[256,1536]{1,0:T(8,128)(2,1)S(1)}, u32[]{:S(2)}, u32[]{:S(2)}) collective-permute-start(bf16[256,1536]{1,0:T(8,128)(2,1)S(1)} %copy-done.4), channel_id=1, source_target_pairs={{0,8},{4,12},{8,0},{12,4},{16,24},{20,28},{24,16},{28,20},{1,9},{5... | collective-permute-start | bytes 2359304 | tf_op jit(solution)/shard_map/ppermute | solution.py:36
  141.9 29.0 %collective-permute-start.32 = (bf16[256,1536]{1,0:T(8,128)(2,1)}, bf16[256,1536]{1,0:T(8,128)(2,1)}, u32[]{:S(2)}, u32[]{:S(2)}) collective-permute-start(bf16[256,1536]{1,0:T(8,128)(2,1)} %get-tuple-element.101.refs_1_), channel_id=1, source_target_pairs={{0,16},{4,20},{8,24},{12,28},{16,0},{20,4},{24,8},{28,12},{1,17},{... | collective-permute-start | bytes 2359304 | tf_op jit(solution)/shard_map/ppermute | solution.py:36
  142.3 31.2 %collective-permute-start.26 = (bf16[256,1536]{1,0:T(8,128)(2,1)}, bf16[256,1536]{1,0:T(8,128)(2,1)S(1)}, u32[]{:S(2)}, u32[]{:S(2)}) collective-permute-start(bf16[256,1536]{1,0:T(8,128)(2,1)} %get-tuple-element.101.refs_1_), channel_id=1, source_target_pairs={{0,8},{4,12},{8,0},{12,4},{16,24},{20,28},{24,16},{28,20},{1,9},{5... | collective-permute-start | bytes 2359304 | tf_op jit(solution)/shard_map/ppermute | solution.py:36
  155.1 20.3 %collective-permute-start.41 = (bf16[128,1536]{1,0:T(8,128)(2,1)S(1)}, bf16[128,1536]{1,0:T(8,128)(2,1)S(1)}, u32[]{:S(2)}, u32[]{:S(2)}) collective-permute-start(bf16[128,1536]{1,0:T(8,128)(2,1)S(1)} %slice.294), channel_id=1, source_target_pairs={{0,8},{4,12},{8,0},{12,4},{16,24},{20,28},{24,16},{28,20},{1,9},{5... | collective-permute-start | bytes 1179656 | tf_op jit(solution)/shard_map/ppermute | solution.py:36
  156.7 22.5 %collective-permute-start.43 = (bf16[128,1536]{1,0:T(8,128)(2,1)S(1)}, bf16[128,1536]{1,0:T(8,128)(2,1)S(1)}, u32[]{:S(2)}, u32[]{:S(2)}) collective-permute-start(bf16[128,1536]{1,0:T(8,128)(2,1)S(1)} %slice.295), channel_id=1, source_target_pairs={{0,16},{4,20},{8,24},{12,28},{16,0},{20,4},{24,8},{28,12},{1,17},{... | collective-permute-start | bytes 1179656 | tf_op jit(solution)/shard_map/ppermute | solution.py:36
  186.2 24.5 %collective-permute-start.24 = (bf16[256,1536]{1,0:T(8,128)(2,1)S(1)}, bf16[256,1536]{1,0:T(8,128)(2,1)}, u32[]{:S(2)}, u32[]{:S(2)}) collective-permute-start(bf16[256,1536]{1,0:T(8,128)(2,1)S(1)} %copy-done.4), channel_id=1, source_target_pairs={{0,4},{4,0},{8,12},{12,8},{16,20},{20,16},{24,28},{28,24},{1,5},{5... | collective-permute-start | bytes 2359304 | tf_op jit(solution)/shard_map/ppermute | solution.py:36
  187.5 23.2 %collective-permute-start.23 = (bf16[256,1536]{1,0:T(8,128)(2,1)}, bf16[256,1536]{1,0:T(8,128)(2,1)}, u32[]{:S(2)}, u32[]{:S(2)}) collective-permute-start(bf16[256,1536]{1,0:T(8,128)(2,1)} %get-tuple-element.101.refs_1_), channel_id=1, source_target_pairs={{0,4},{4,0},{8,12},{12,8},{16,20},{20,16},{24,28},{28,24},{1,5},{5... | collective-permute-start | bytes 2359304 | tf_op jit(solution)/shard_map/ppermute | solution.py:36
  188.2 34.2 %collective-permute-start.29 = (bf16[256,1536]{1,0:T(8,128)(2,1)S(1)}, bf16[256,1536]{1,0:T(8,128)(2,1)}, u32[]{:S(2)}, u32[]{:S(2)}) collective-permute-start(bf16[256,1536]{1,0:T(8,128)(2,1)S(1)} %collective-permute-done.28.refs_3_.refs_7_), channel_id=1, source_target_pairs={{0,4},{4,0},{8,12},{12,8},{16,20},{20,16},{24,28},{28,24},{1,5},{5... | collective-permute-start | bytes 2359304 | tf_op jit(solution)/shard_map/ppermute | solution.py:36
  189.5 45.3 %collective-permute-start.35 = (bf16[256,1536]{1,0:T(8,128)(2,1)}, bf16[256,1536]{1,0:T(8,128)(2,1)}, u32[]{:S(2)}, u32[]{:S(2)}) collective-permute-start(bf16[256,1536]{1,0:T(8,128)(2,1)} %collective-permute-done.34.refs_3_.refs_13_), channel_id=1, source_target_pairs={{0,4},{4,0},{8,12},{12,8},{16,20},{20,16},{24,28},{28,24},{1,5},{5... | collective-permute-start | bytes 2359304 | tf_op jit(solution)/shard_map/ppermute | solution.py:36
  190.3 32.2 %collective-permute-start.27 = (bf16[256,1536]{1,0:T(8,128)(2,1)S(1)}, bf16[256,1536]{1,0:T(8,128)(2,1)}, u32[]{:S(2)}, u32[]{:S(2)}) collective-permute-start(bf16[256,1536]{1,0:T(8,128)(2,1)S(1)} %collective-permute-done.26.refs_1_.refs_3_), channel_id=1, source_target_pairs={{0,4},{4,0},{8,12},{12,8},{16,20},{20,16},{24,28},{28,24},{1,5},{5... | collective-permute-start | bytes 2359304 | tf_op jit(solution)/shard_map/ppermute | solution.py:36
  210.7 24.1 %collective-permute-start.33 = (bf16[256,1536]{1,0:T(8,128)(2,1)}, bf16[256,1536]{1,0:T(8,128)(2,1)S(1)}, u32[]{:S(2)}, u32[]{:S(2)}) collective-permute-start(bf16[256,1536]{1,0:T(8,128)(2,1)} %collective-permute-done.32.refs_1_.refs_9_), channel_id=1, source_target_pairs={{0,4},{4,0},{8,12},{12,8},{16,20},{20,16},{24,28},{28,24},{1,5},{5... | collective-permute-start | bytes 2359304 | tf_op jit(solution)/shard_map/ppermute | solution.py:36
  210.7 22.0 %collective-permute-start.45 = (bf16[256,1536]{1,0:T(8,128)(2,1)S(1)}, bf16[256,1536]{1,0:T(8,128)(2,1)S(1)}, u32[]{:S(2)}, u32[]{:S(2)}) collective-permute-start(bf16[256,1536]{1,0:T(8,128)(2,1)S(1)} %get-tuple-element.114), channel_id=1, source_target_pairs={{0,4},{4,0},{8,12},{12,8},{16,20},{20,16},{24,28},{28,24},{1,5},{5... | collective-permute-start | bytes 2359304 | tf_op jit(solution)/shard_map/ppermute | solution.py:36
  232.4 25.9 %collective-permute-start.30 = (bf16[256,1536]{1,0:T(8,128)(2,1)}, bf16[256,1536]{1,0:T(8,128)(2,1)}, u32[]{:S(2)}, u32[]{:S(2)}) collective-permute-start(bf16[256,1536]{1,0:T(8,128)(2,1)} %get-tuple-element.110), channel_id=1, source_target_pairs={{0,4},{4,0},{8,12},{12,8},{16,20},{20,16},{24,28},{28,24},{1,5},{5... | collective-permute-start | bytes 2359304 | tf_op jit(solution)/shard_map/ppermute | solution.py:36
  234.1 24.2 %collective-permute-start.48 = (bf16[128,1536]{1,0:T(8,128)(2,1)}, bf16[128,1536]{1,0:T(8,128)(2,1)}, u32[]{:S(2)}, u32[]{:S(2)}) collective-permute-start(bf16[128,1536]{1,0:T(8,128)(2,1)} %get-tuple-element.189), channel_id=1, source_target_pairs={{0,16},{4,20},{8,24},{12,28},{16,0},{20,4},{24,8},{28,12},{1,17},{... | collective-permute-start | bytes 1179656 | tf_op jit(solution)/shard_map/ppermute | solution.py:36
  256.2 174.0 %reduce-scatter.7.cloned.1.call-start = ((), (), s32[]{:S(2)}) async-start(), calls=%async_computation.8 | async-start | bytes 737280 | tf_op jit(solution)/shard_map/reduce_scatter | solution.py:554
  296.5 29.0 %collective-permute-start.51 = (bf16[256,1536]{1,0:T(8,128)(2,1)}, bf16[256,1536]{1,0:T(8,128)(2,1)S(1)}, u32[]{:S(2)}, u32[]{:S(2)}) collective-permute-start(bf16[256,1536]{1,0:T(8,128)(2,1)} %get-tuple-element.116.refs_1_.refs_5_), channel_id=1, source_target_pairs={{0,4},{4,0},{8,12},{12,8},{16,20},{20,16},{24,28},{28,24},{1,5},{5... | collective-permute-start | bytes 2359304 | tf_op jit(solution)/shard_map/ppermute | solution.py:36
  335.8 193.2 %reduce-scatter.5.cloned.1.call-start = ((), (), s32[]{:S(2)}) async-start(), calls=%async_computation.7 | async-start | bytes 1474560 | tf_op jit(solution)/shard_map/reduce_scatter | solution.py:554
  384.1 159.7 %reduce-scatter.9.cloned.1.call-start = ((), (), s32[]{:S(2)}) async-start(), calls=%async_computation.9 | async-start | bytes 3932160 | tf_op jit(solution)/shard_map/reduce_scatter | solution.py:554
  398.4 70.1 %collective-permute-start.70 = (bf16[256,1536]{1,0:T(8,128)(2,1)}, bf16[256,1536]{1,0:T(8,128)(2,1)}, u32[]{:S(2)}, u32[]{:S(2)}) collective-permute-start(bf16[256,1536]{1,0:T(8,128)(2,1)} %get-tuple-element.134), channel_id=1, source_target_pairs={{0,4},{4,0},{8,12},{12,8},{16,20},{20,16},{24,28},{28,24},{1,5},{5... | collective-permute-start | bytes 2359304 | tf_op jit(solution)/shard_map/ppermute | solution.py:36
  399.6 23.4 %collective-permute-start.64 = (bf16[256,1536]{1,0:T(8,128)(2,1)S(1)}, bf16[256,1536]{1,0:T(8,128)(2,1)S(1)}, u32[]{:S(2)}, u32[]{:S(2)}) collective-permute-start(bf16[256,1536]{1,0:T(8,128)(2,1)S(1)} %copy-done.17), channel_id=1, source_target_pairs={{0,4},{4,0},{8,12},{12,8},{16,20},{20,16},{24,28},{28,24},{1,5},{5... | collective-permute-start | bytes 2359304 | tf_op jit(solution)/shard_map/ppermute | solution.py:36
  400.1 28.3 %collective-permute-start.61 = (bf16[256,1536]{1,0:T(8,128)(2,1)}, bf16[256,1536]{1,0:T(8,128)(2,1)S(1)}, u32[]{:S(2)}, u32[]{:S(2)}) collective-permute-start(bf16[256,1536]{1,0:T(8,128)(2,1)} %copy-done.18), channel_id=1, source_target_pairs={{0,4},{4,0},{8,12},{12,8},{16,20},{20,16},{24,28},{28,24},{1,5},{5... | collective-permute-start | bytes 2359304 | tf_op jit(solution)/shard_map/ppermute | solution.py:36
  400.2 25.8 %collective-permute-start.74 = (bf16[256,1536]{1,0:T(8,128)(2,1)}, bf16[256,1536]{1,0:T(8,128)(2,1)S(1)}, u32[]{:S(2)}, u32[]{:S(2)}) collective-permute-start(bf16[256,1536]{1,0:T(8,128)(2,1)} %get-tuple-element.143), channel_id=1, source_target_pairs={{0,4},{4,0},{8,12},{12,8},{16,20},{20,16},{24,28},{28,24},{1,5},{5... | collective-permute-start | bytes 2359304 | tf_op jit(solution)/shard_map/ppermute | solution.py:36
  440.3 28.3 %collective-permute-start.60 = (bf16[256,1536]{1,0:T(8,128)(2,1)S(1)}, bf16[256,1536]{1,0:T(8,128)(2,1)S(1)}, u32[]{:S(2)}, u32[]{:S(2)}) collective-permute-start(bf16[256,1536]{1,0:T(8,128)(2,1)S(1)} %copy-done.15), channel_id=1, source_target_pairs={{0,4},{4,0},{8,12},{12,8},{16,20},{20,16},{24,28},{28,24},{1,5},{5... | collective-permute-start | bytes 2359304 | tf_op jit(solution)/shard_map/ppermute | solution.py:36
  442.2 28.2 %collective-permute-start.73 = (bf16[256,1536]{1,0:T(8,128)(2,1)S(1)}, bf16[256,1536]{1,0:T(8,128)(2,1)S(1)}, u32[]{:S(2)}, u32[]{:S(2)}) collective-permute-start(bf16[256,1536]{1,0:T(8,128)(2,1)S(1)} %copy-done.92), channel_id=1, source_target_pairs={{0,4},{4,0},{8,12},{12,8},{16,20},{20,16},{24,28},{28,24},{1,5},{5... | collective-permute-start | bytes 2359304 | tf_op jit(solution)/shard_map/ppermute | solution.py:36
  444.0 20.3 %collective-permute-start.93 = (bf16[48,1536]{1,0:T(8,128)(2,1)S(1)}, bf16[48,1536]{1,0:T(8,128)(2,1)S(1)}, u32[]{:S(2)}, u32[]{:S(2)}) collective-permute-start(bf16[48,1536]{1,0:T(8,128)(2,1)S(1)} %collective-permute-done.89), channel_id=1, source_target_pairs={{0,16},{4,20},{8,24},{12,28},{16,0},{20,4},{24,8},{28,12},{1,17},{... | collective-permute-start | bytes 442376 | tf_op jit(solution)/shard_map/ppermute | solution.py:36
  468.5 32.5 %collective-permute-start.62 = (bf16[128,1536]{1,0:T(8,128)(2,1)S(1)}, bf16[128,1536]{1,0:T(8,128)(2,1)S(1)}, u32[]{:S(2)}, u32[]{:S(2)}) collective-permute-start(bf16[128,1536]{1,0:T(8,128)(2,1)S(1)} %get-tuple-element.182), channel_id=1, source_target_pairs={{0,8},{4,12},{8,0},{12,4},{16,24},{20,28},{24,16},{28,20},{1,9},{5... | collective-permute-start | bytes 1179656 | tf_op jit(solution)/shard_map/ppermute | solution.py:36
  468.7 33.0 %collective-permute-start.66 = (bf16[128,1536]{1,0:T(8,128)(2,1)S(1)}, bf16[128,1536]{1,0:T(8,128)(2,1)S(1)}, u32[]{:S(2)}, u32[]{:S(2)}) collective-permute-start(bf16[128,1536]{1,0:T(8,128)(2,1)S(1)} %get-tuple-element.180), channel_id=1, source_target_pairs={{0,16},{4,20},{8,24},{12,28},{16,0},{20,4},{24,8},{28,12},{1,17},{... | collective-permute-start | bytes 1179656 | tf_op jit(solution)/shard_map/ppermute | solution.py:36
  470.4 32.1 %collective-permute-start.68 = (bf16[128,1536]{1,0:T(8,128)(2,1)S(1)}, bf16[128,1536]{1,0:T(8,128)(2,1)S(1)}, u32[]{:S(2)}, u32[]{:S(2)}) collective-permute-start(bf16[128,1536]{1,0:T(8,128)(2,1)S(1)} %get-tuple-element.181), channel_id=1, source_target_pairs={{0,8},{4,12},{8,0},{12,4},{16,24},{20,28},{24,16},{28,20},{1,9},{5... | collective-permute-start | bytes 1179656 | tf_op jit(solution)/shard_map/ppermute | solution.py:36
  480.4 24.9 %collective-permute-start.69 = (bf16[128,1536]{1,0:T(8,128)(2,1)S(1)}, bf16[128,1536]{1,0:T(8,128)(2,1)S(1)}, u32[]{:S(2)}, u32[]{:S(2)}) collective-permute-start(bf16[128,1536]{1,0:T(8,128)(2,1)S(1)} %get-tuple-element.179), channel_id=1, source_target_pairs={{0,16},{4,20},{8,24},{12,28},{16,0},{20,4},{24,8},{28,12},{1,17},{... | collective-permute-start | bytes 1179656 | tf_op jit(solution)/shard_map/ppermute | solution.py:36
  505.3 22.0 %collective-permute-start.92 = (bf16[48,1536]{1,0:T(8,128)(2,1)}, bf16[48,1536]{1,0:T(8,128)(2,1)}, u32[]{:S(2)}, u32[]{:S(2)}) collective-permute-start(bf16[48,1536]{1,0:T(8,128)(2,1)} %collective-permute-done.91), channel_id=1, source_target_pairs={{0,4},{4,0},{8,12},{12,8},{16,20},{20,16},{24,28},{28,24},{1,5},{5... | collective-permute-start | bytes 442376 | tf_op jit(solution)/shard_map/ppermute | solution.py:36
  543.8 20.2 %collective-permute-start.100 = (bf16[384,1024]{1,0:T(8,128)(2,1)}, bf16[384,1024]{1,0:T(8,128)(2,1)S(1)}, u32[]{:S(2)}, u32[]{:S(2)}) collective-permute-start(bf16[384,1024]{1,0:T(8,128)(2,1)} %reduce-scatter.9.cloned.1.call-done), channel_id=1, source_target_pairs={{0,8},{4,12},{8,0},{12,4},{16,24},{20,28},{24,16},{28,20},{1,9},{5... | collective-permute-start | bytes 2359304 | tf_op jit(solution)/shard_map/ppermute | solution.py:36
  548.2 23.2 %collective-permute-start.102 = (bf16[384,1024]{1,0:T(8,128)(2,1)}, bf16[384,1024]{1,0:T(8,128)(2,1)}, u32[]{:S(2)}, u32[]{:S(2)}) collective-permute-start(bf16[384,1024]{1,0:T(8,128)(2,1)} %reduce-scatter.9.cloned.1.call-done), channel_id=1, source_target_pairs={{0,16},{4,20},{8,24},{12,28},{16,0},{20,4},{24,8},{28,12},{1,17},{... | collective-permute-start | bytes 2359304 | tf_op jit(solution)/shard_map/ppermute | solution.py:36
  550.6 27.3 %collective-permute-start.99 = (bf16[384,1024]{1,0:T(8,128)(2,1)}, bf16[384,1024]{1,0:T(8,128)(2,1)}, u32[]{:S(2)}, u32[]{:S(2)}) collective-permute-start(bf16[384,1024]{1,0:T(8,128)(2,1)} %reduce-scatter.9.cloned.1.call-done), channel_id=1, source_target_pairs={{0,4},{4,0},{8,12},{12,8},{16,20},{20,16},{24,28},{28,24},{1,5},{5... | collective-permute-start | bytes 2359304 | tf_op jit(solution)/shard_map/ppermute | solution.py:36
  563.9 21.3 %collective-permute-start.101 = (bf16[384,1024]{1,0:T(8,128)(2,1)S(1)}, bf16[384,1024]{1,0:T(8,128)(2,1)}, u32[]{:S(2)}, u32[]{:S(2)}) collective-permute-start(bf16[384,1024]{1,0:T(8,128)(2,1)S(1)} %collective-permute-done.100), channel_id=1, source_target_pairs={{0,4},{4,0},{8,12},{12,8},{16,20},{20,16},{24,28},{28,24},{1,5},{5... | collective-permute-start | bytes 2359304 | tf_op jit(solution)/shard_map/ppermute | solution.py:36
  (171 other events, 1607.4 us)
Sparse Core Ops, SparseCore 0:
  12.1 38.8 all-gather.3
  52.6 42.5 all-gather.7
  96.8 62.2 all-gather.5
  256.3 33.9 reduce-scatter.10
  335.9 21.0 reduce-scatter.6
  384.2 28.2 reduce-scatter.4
  415.3 67.8 reduce-scatter.8
where the time goes:
time: 631 us; the launch traced here: 626 us
  waiting for transfers between devices  202 us (32%)
  Pallas kernels  186 us (29%)
  starting transfers between devices  108 us (17%)
  local copies, waits for them, and re-layouts  88.1 us (14%)
  other arithmetic  24.3 us (4%)
  between operations  15.6 us (2%)
    ppermute x112, waiting for transfers between devices, swap(): return lax.ppermute(x, 'replica', [(i, i ^ bit) for i in range(size)])  201 us
    pallas_call x16, Pallas kernels, call(): pl.pallas_call(kernel, out_shape=outputs, scratch_shapes=list(scratch), c...  120 us
    ppermute x112, starting transfers between devices, swap(): return lax.ppermute(x, 'replica', [(i, i ^ bit) for i in range(size)])  94.8 us
    unnamed x236, local copies, waits for them, and re-layouts  68.3 us
    pallas_call x4, Pallas kernels, grads_call(): pl.pallas_call(kernel, grid=(width // tile,), in_specs=specs, out_specs=o...  37.9 us
    pallas_call x1, Pallas kernels, spread(): pl.pallas_call(spread_kernel, grid_spec=spec, out_shape=[jax.ShapeDtypeSt...  23.4 us
  transfers between devices with their start and end apart: 124, of which 44 were waited for; matrix products, arithmetic and copies ran while one was open for 11% of the time, Pallas kernels for 26%

commit v1 on v0

--- a/solution.py
+++ b/solution.py
@@ -13,7 +13,7 @@
 LANES = 128
 NORM_EPS = 1e-05
 ROPE_BASE = 100000.0
-VMEM_BYTES = 60 * 1024 * 1024
+VMEM_BYTES = 40 * 1024 * 1024
 MLP_VMEM_BYTES = 40 * 1024 * 1024
 F32 = jnp.float32
 BF16 = jnp.bfloat16
@@ -440,98 +440,150 @@
     )
 
 
-def spread_kernel(at_ref, gate_ref, up_ref, down_ref, wg_ref, wu_ref, gate_out, up_out, down_out, gain_out):
-    gate, upward = gate_ref[0].astype(F32), up_ref[0].astype(F32)
-    gate_out[...] = gate
-    up_out[...] = upward
-    down_out[...] = down_ref[0].astype(F32)
-
-    @pl.when((pl.program_id(0) == 0) & (pl.program_id(1) == 0))
+def spread_wide_kernel(counts, at_ref, *refs):
+    blocks, (wg_ref, wu_ref, gate_out, up_out, gain_out) = take(refs, counts)
+    j, part = pl.program_id(0), pl.program_id(1)
+    tile, parts = gate_out.shape[1], pl.num_programs(1)
+
+    @pl.when((j == 0) & (part == 0))
     def _():
         gain_out[...] = jnp.zeros_like(gain_out)
 
-    gain_out[...] += gate * wg_ref[...].astype(F32) + upward * wu_ref[...].astype(F32)
-
-
-def spread(at, gate_up, down, w_gate, w_up, parts):
-    count, width, wide = gate_up.shape
-    tile = wide // 2 // parts
-    short = down.shape[1] // parts
-    columns = pl.BlockSpec((width, tile), lambda a, s, at: (0, s * count + a))
-    spec = pltpu.PrefetchScalarGridSpec(
-        num_scalar_prefetch=1,
-        grid=(count, parts),
-        in_specs=[
-            pl.BlockSpec((1, width, tile), lambda a, s, at: (a ^ at[0], 0, s)),
-            pl.BlockSpec((1, width, tile), lambda a, s, at: (a ^ at[0], 0, parts + s)),
-            pl.BlockSpec((1, short, down.shape[2]), lambda a, s, at: (a ^ at[0], s, 0)),
-            columns,
-            columns,
-        ],
-        out_specs=[
-            columns,
-            columns,
-            pl.BlockSpec((short, down.shape[2]), lambda a, s, at: (a * parts + s, 0)),
-            pl.BlockSpec((width, tile), lambda a, s, at: (0, 0)),
-        ],
-    )
+    here = pl.multiple_of(part * tile, tile)
+    over = pl.multiple_of((parts + part) * tile, tile)
+    for k, block in enumerate(blocks):
+
+        @pl.when(j == k)
+        def _(block=block):
+            at = 0
+            for piece in block:
+                rows = slice(at, at + piece.shape[0])
+                gate_out[rows, :] = piece[:, pl.ds(here, tile)].astype(F32)
+                up_out[rows, :] = piece[:, pl.ds(over, tile)].astype(F32)
+                at += piece.shape[0]
+
+    gain_out[...] += gate_out[...] * wg_ref[...].astype(F32) + up_out[...] * wu_ref[...].astype(F32)
+
+
+def spread_wide(at, blocks, w_gate, w_up, parts):
+    counts, pieces, count = [len(b) for b in blocks], flat(blocks), len(blocks)
+    width, total = w_gate.shape
+    tile = total // count // parts
+    columns = pl.BlockSpec((width, tile), lambda j, s, at: (0, s * count + (j ^ at[0])))
     return pl.pallas_call(
-        spread_kernel,
-        grid_spec=spec,
+        functools.partial(spread_wide_kernel, counts),
+        grid_spec=pltpu.PrefetchScalarGridSpec(
+            num_scalar_prefetch=1,
+            grid=(count, parts),
+            in_specs=[
+                pl.BlockSpec(p.shape, lambda j, s, at: (0, 0), pipeline_mode=pl.Buffered(1))
+                for p in pieces
+            ]
+            + [columns, columns],
+            out_specs=[columns, columns, pl.BlockSpec((width, tile), lambda j, s, at: (0, 0))],
+        ),
         out_shape=[
-            jax.ShapeDtypeStruct((width, count * wide // 2), F32),
-            jax.ShapeDtypeStruct((width, count * wide // 2), F32),
-            jax.ShapeDtypeStruct((count * down.shape[1], down.shape[2]), F32),
+            jax.ShapeDtypeStruct((width, total), F32),
+            jax.ShapeDtypeStruct((width, total), F32),
             jax.ShapeDtypeStruct((width, tile), F32),
         ],
-        compiler_params=pltpu.CompilerParams(dimension_semantics=("arbitrary", "arbitrary")),
-        cost_estimate=pl.CostEstimate(
-            flops=0, bytes_accessed=6 * (gate_up.size + down.size), transcendentals=0
+        compiler_params=pltpu.CompilerParams(
+            dimension_semantics=("arbitrary", "arbitrary"), vmem_limit_bytes=VMEM_BYTES
         ),
-        name="spread",
-    )(at, gate_up, gate_up, down, w_gate, w_up)
-
-
-def spread_attn_kernel(count, cuts, at_ref, *refs):
-    blocks, (wq_ref, wk_ref, wv_ref), (q_out, k_out, v_out, gain_out) = refs[:count], refs[count : count + 3], refs[count + 3 :]
-
-    @pl.when(pl.program_id(0) == 0)
+        cost_estimate=pl.CostEstimate(flops=0, bytes_accessed=16 * width * total, transcendentals=0),
+        name="spread_wide",
+    )(at, *pieces, w_gate, w_up)
+
+
+def spread_rows_kernel(counts, at_ref, *refs):
+    blocks, (down_out, o_out) = take(refs, counts)
+    j, short = pl.program_id(0), down_out.shape[0]
+    for k, block in enumerate(blocks):
+
+        @pl.when(j == k)
+        def _(block=block):
+            values = load(block).astype(F32)
+            down_out[...] = values[:short]
+            o_out[...] = values[short:]
+
+
+def spread_rows(at, blocks, short):
+    counts, pieces, count = [len(b) for b in blocks], flat(blocks), len(blocks)
+    rows, width = sum(p.shape[0] for p in blocks[0]), pieces[0].shape[1]
+    place = lambda j, at: (j ^ at[0], 0)
+    return pl.pallas_call(
+        functools.partial(spread_rows_kernel, counts),
+        grid_spec=pltpu.PrefetchScalarGridSpec(
+            num_scalar_prefetch=1,
+            grid=(count,),
+            in_specs=[
+                pl.BlockSpec(p.shape, lambda j, at: (0, 0), pipeline_mode=pl.Buffered(1))
+                for p in pieces
+            ],
+            out_specs=[pl.BlockSpec((short, width), place), pl.BlockSpec((rows - short, width), place)],
+        ),
+        out_shape=[
+            jax.ShapeDtypeStruct((count * short, width), F32),
+            jax.ShapeDtypeStruct((count * (rows - short), width), F32),
+        ],
+        compiler_params=pltpu.CompilerParams(
+            dimension_semantics=("arbitrary",), vmem_limit_bytes=VMEM_BYTES
+        ),
+        cost_estimate=pl.CostEstimate(flops=0, bytes_accessed=6 * count * rows * width, transcendentals=0),
+        name="spread_rows",
+    )(at, *pieces)
+
+
+def spread_attn_kernel(counts, count, cuts, at_ref, *refs):
+    blocks, rest = take(refs, counts)
+    (wq_ref, wk_ref, wv_ref), (q_out, k_out, v_out, gain_out, stack) = rest[:3], rest[3:]
+    step = pl.program_id(0)
+
+    @pl.when(step == 0)
     def _():
         gain_out[...] = jnp.zeros_like(gain_out)
+        for j, block in enumerate(blocks):
+            stack[j ^ at_ref[0]] = load(block)
 
     total = 0.0
-    spans = ((0, cuts[0]), (cuts[0], cuts[1]), (cuts[1], blocks[0].shape[2]))
+    spans = ((0, cuts[0]), (cuts[0], cuts[1]), (cuts[1], stack.shape[2]))
+    held = [stack[step * count + i].astype(F32) for i in range(count)]
     for (low, high), out, w_ref in zip(spans, (q_out, k_out, v_out), (wq_ref, wk_ref, wv_ref)):
-        made = jnp.concatenate([b[0, :, low:high].astype(F32) for b in blocks], 1)
+        made = jnp.concatenate([b[:, low:high] for b in held], 1)
         out[...] = made
         total += jnp.sum(made * w_ref[...].astype(F32), 1, keepdims=True)
     gain_out[...] += total
 
 
-def spread_attn(at, stack, weights, cuts):
-    group, slab, narrow = stack.shape
-    count = LANES // math.gcd(LANES, HEAD_DIM)
-    count = math.gcd(group, count)
+def spread_attn(at, blocks, weights, cuts):
+    counts, pieces, group = [len(b) for b in blocks], flat(blocks), len(blocks)
+    slab, narrow = weights[0].shape[0], pieces[0].shape[1]
+    count = math.gcd(group, LANES // math.gcd(LANES, HEAD_DIM))
     widths = (cuts[0], cuts[1] - cuts[0], narrow - cuts[1])
     columns = [pl.BlockSpec((slab, count * w), lambda p, at: (0, p)) for w in widths]
-
-    def block(i):
-        return pl.BlockSpec((1, slab, narrow), lambda p, at: ((p * count + i) ^ at[0], 0, 0))
-
     return pl.pallas_call(
-        functools.partial(spread_attn_kernel, count, cuts),
+        functools.partial(spread_attn_kernel, counts, count, cuts),
         grid_spec=pltpu.PrefetchScalarGridSpec(
             num_scalar_prefetch=1,
             grid=(group // count,),
-            in_specs=[block(i) for i in range(count)] + columns,
+            in_specs=[
+                pl.BlockSpec(p.shape, lambda p_, at: (0, 0), pipeline_mode=pl.Buffered(1))
+                for p in pieces
+            ]
+            + columns,
             out_specs=columns + [pl.BlockSpec((slab, 1), lambda p, at: (0, 0))],
+            scratch_shapes=[pltpu.VMEM((group, slab, narrow), BF16)],
         ),
         out_shape=[jax.ShapeDtypeStruct((slab, group * w), F32) for w in widths]
         + [jax.ShapeDtypeStruct((slab, 1), F32)],
-        compiler_params=pltpu.CompilerParams(dimension_semantics=("arbitrary",)),
-        cost_estimate=pl.CostEstimate(flops=0, bytes_accessed=8 * stack.size, transcendentals=0),
+        compiler_params=pltpu.CompilerParams(
+            dimension_semantics=("arbitrary",), vmem_limit_bytes=VMEM_BYTES
+        ),
+        cost_estimate=pl.CostEstimate(
+            flops=0, bytes_accessed=8 * group * slab * narrow, transcendentals=0
+        ),
         name="spread_attn",
-    )(at, *[stack] * count, *weights)
+    )(at, *pieces, *weights)
 
 
 def head_columns(queries, keys):
@@ -666,7 +718,7 @@
         all_c, acrosses, [], wd.shape, 1, 2 * rows * width * wd.shape[0],
         (wd.shape[0], rows),
     )
-    g_gu, g_d = scatter_shard(g_gu), scatter_shard(g_d)
+    g_gu = scatter_shard(g_gu)
     dm = plane_gather(dm_own, high)
     all_dm = flat(dm[k] for j in order for k in (j ^ 1, j))
     g_o = grads_call(
@@ -674,7 +726,10 @@
         all_dm, [saved[j][2] for j in order], [], wo.shape, 1,
         2 * rows * width * wo.shape[0],
     )
-    g_o = lax.ppermute(scatter_shard(g_o), ("replica", "shard"), back)
+    g_rows = [g.reshape(shards, -1, width) for g in (g_d, g_o)]
+    g_rows = scatter_shard(jnp.concatenate(g_rows, 1).reshape(-1, width))
+    g_o = lax.ppermute(g_rows[hidden:], ("replica", "shard"), back)
+    g_rows = jnp.concatenate([g_rows[:hidden], g_o], 0)
 
     das, dqkvs = {}, []
     for j in order:
@@ -695,22 +750,20 @@
 
     bit = group
     while bit < replicas:
-        g_gu, g_d, g_w, g_o = (g + swap(g, bit) for g in (g_gu, g_d, g_w, g_o))
+        g_gu, g_rows, g_w = (g + swap(g, bit) for g in (g_gu, g_rows, g_w))
         bit *= 2
 
-    def stacked(g):
+    def blocks(g):
         got = plane_gather(g, high)
-        return jnp.concatenate(flat(got[j] for j in range(group)), 0).reshape(group, *g.shape)
-
-    gate_grad, up_grad, down_grad, gain_terms = spread(
-        place.reshape(1), stacked(g_gu), stacked(g_d), w_gate, w_up, shards
-    )
+        return [got[j] for j in range(group)]
+
+    here = place.reshape(1)
+    gate_grad, up_grad, gain_terms = spread_wide(here, blocks(g_gu), w_gate, w_up, shards)
     mlp_gain_grad = jnp.sum(gain_terms, 1) / mlp_gain.astype(F32)
-    absolute = jnp.arange(group) ^ place
-    out_grad = stacked(g_o)[absolute].astype(F32).reshape(group * chunk, width)
+    down_grad, out_grad = spread_rows(here, blocks(g_rows), hidden)
     cuts = (queries * HEAD_DIM, (queries + keys) * HEAD_DIM)
     query_grad, key_grad, value_grad, gain_terms = spread_attn(
-        place.reshape(1), stacked(g_w), (w_query, w_key, w_value), cuts
+        here, blocks(g_w), (w_query, w_key, w_value), cuts
     )
     attn_gain_grad = gain_terms[:, 0] / attn_gain.astype(F32)
     return (

time: 631 us -> 590 us (0.935)
  Pallas kernels: 186 us -> 139 us
  local copies, waits for them, and re-layouts: 88.1 us -> 112 us
  starting transfers between devices: 108 us -> 91.9 us
  other arithmetic: 24.3 us -> 16.6 us
  waiting for transfers between devices: 202 us -> 209 us
    pallas_call x16, Pallas kernels: 120 us -> 84.1 us  [call(): pl.pallas_call(kernel, out_shape=outputs, scratch_shapes=list(scratch), c...]
    ppermute x112 -> x103, starting transfers between devices: 94.8 us -> 78.1 us  [swap(): return lax.ppermute(x, 'replica', [(i, i ^ bit) for i in range(size)])]
    unnamed x236 -> x356, local copies, waits for them, and re-layouts: 68.3 us -> 84.8 us
    pallas_call x4, Pallas kernels: 37.9 us -> 26.9 us  [grads_call(): pl.pallas_call(kernel, grid=(width // tile,), in_specs=specs, out_specs=o...]
    ppermute x112 -> x103, waiting for transfers between devices: 201 us -> 209 us  [swap(): return lax.ppermute(x, 'replica', [(i, i ^ bit) for i in range(size)])]
    slice x16 -> x14, local copies, waits for them, and re-layouts: 8.36 us -> 14 us  [plane_gather(): far = (swap(from_b[:cut], a), swap(from_a[cut:], b))]
    pallas_call x2 -> x3, Pallas kernels: 28.3 us -> 27.9 us  [the longest x1 16 us: spread_wide(): pl.pallas_call(functools.partial(spread_wide_kernel, counts), grid_spec=p...]
  transfers between devices with their start and end apart: 124 -> 114, of which waited for: 44 -> 40; matrix products, arithmetic and copies ran while one was open for 11% -> 8% of each run, Pallas kernels for 26% -> 19%
where the time goes in v1:
time: 590 us; the launch traced here: 586 us
  waiting for transfers between devices  209 us (35%)
  Pallas kernels  139 us (24%)
  local copies, waits for them, and re-layouts  112 us (19%)
  starting transfers between devices  91.9 us (16%)
  other arithmetic  16.6 us (3%)
  between operations  16.1 us (3%)
    ppermute x103, waiting for transfers between devices, swap(): return lax.ppermute(x, 'replica', [(i, i ^ bit) for i in range(size)])  209 us
    unnamed x356, local copies, waits for them, and re-layouts  84.8 us
    pallas_call x16, Pallas kernels, call(): pl.pallas_call(kernel, out_shape=outputs, scratch_shapes=list(scratch), c...  84.1 us
    ppermute x103, starting transfers between devices, swap(): return lax.ppermute(x, 'replica', [(i, i ^ bit) for i in range(size)])  78.1 us
    pallas_call x4, Pallas kernels, grads_call(): pl.pallas_call(kernel, grid=(width // tile,), in_specs=specs, out_specs=o...  26.9 us
    pallas_call x1, Pallas kernels, spread_wide(): pl.pallas_call(functools.partial(spread_wide_kernel, counts), grid_spec=p...  16 us
    slice x14, local copies, waits for them, and re-layouts, plane_gather(): far = (swap(from_b[:cut], a), swap(from_a[cut:], b))  14 us
    ppermute x4, starting transfers between devices, layer(): came.append(lax.ppermute(mine, ('replica', 'shard'), route))  12.5 us
  transfers between devices with their start and end apart: 114, of which 40 were waited for; matrix products, arithmetic and copies ran while one was open for 8% of the time, Pallas kernels for 19%

profile of v1, /device:TPU:0, one launch (start us, length us, event | category | flops | bytes accessed | tf_op | source)
XLA Modules:
  0.0 585.5 jit_solution(4939168739904250096)
XLA Ops:
  14.5 7.0 %collective-permute-start.4 = (bf16[48,1536]{1,0:T(8,128)(2,1)}, bf16[48,1536]{1,0:T(8,128)(2,1)S(1)}, u32[]{:S(2)}, u32[]{:S(2)}) collective-permute-start(bf16[48,1536]{1,0:T(8,128)(2,1)} %constant_dynamic-slice_fusion.1), channel_id=1, source_target_pairs={{0,3},{1,11},{2,19},{3,27},{4,0},{5,8},{6,16},{7,24},{8,1},{9,9},{... | collective-permute-start | bytes 442376 | tf_op jit(solution)/shard_map/ppermute | solution.py:657
  37.8 9.6 %collective-permute-done.10.refs_1_ = bf16[256,1536]{1,0:T(8,128)(2,1)S(1)} collective-permute-done((bf16[256,1536]{1,0:T(8,128)(2,1)}, bf16[256,1536]{1,0:T(8,128)(2,1)S(1)}, u32[]{:S(2)}, u32[]{:S(2)}) %collective-permute-start.10) | collective-permute-done | bytes 786464 | tf_op jit(solution)/shard_map/ppermute | solution.py:36
  49.2 3.2 collective-permute-start.13
  58.0 6.8 %collective-permute-done.13.refs_2_ = bf16[128,1536]{1,0:T(8,128)(2,1)S(1)} collective-permute-done((bf16[128,1536]{1,0:T(8,128)(2,1)S(1)}, bf16[128,1536]{1,0:T(8,128)(2,1)S(1)}, u32[]{:S(2)}, u32[]{:S(2)}) %collective-permute-start.13) | collective-permute-done | bytes 393248 | tf_op jit(solution)/shard_map/ppermute | solution.py:36
  74.2 3.4 shard_map.197
  80.9 4.8 shard_map.195
  88.5 3.4 shard_map.196
  94.3 3.6 shard_map.194
  101.7 9.6 %collective-permute-done.18 = bf16[128,1536]{1,0:T(8,128)(2,1)S(1)} collective-permute-done((bf16[128,1536]{1,0:T(8,128)(2,1)S(1)}, bf16[128,1536]{1,0:T(8,128)(2,1)S(1)}, u32[]{:S(2)}, u32[]{:S(2)}) %collective-permute-start.18) | collective-permute-done | bytes 393248 | tf_op jit(solution)/shard_map/ppermute | solution.py:36
  115.7 4.0 collective-permute-done.9.refs_2_
  123.8 4.3 collective-permute-done.21.refs_4_
  128.1 3.8 collective-permute-done.22.refs_5_
  136.4 8.7 %collective-permute-done.28.refs_3_.refs_7_ = bf16[256,1536]{1,0:T(8,128)(2,1)} collective-permute-done((bf16[256,1536]{1,0:T(8,128)(2,1)S(1)}, bf16[256,1536]{1,0:T(8,128)(2,1)}, u32[]{:S(2)}, u32[]{:S(2)}) %collective-permute-start.28) | collective-permute-done | bytes 786464 | tf_op jit(solution)/shard_map/ppermute | solution.py:36
  145.1 16.5 %collective-permute-done.26.refs_1_.refs_3_ = bf16[256,1536]{1,0:T(8,128)(2,1)} collective-permute-done((bf16[256,1536]{1,0:T(8,128)(2,1)S(1)}, bf16[256,1536]{1,0:T(8,128)(2,1)}, u32[]{:S(2)}, u32[]{:S(2)}) %collective-permute-start.26) | collective-permute-done | bytes 786464 | tf_op jit(solution)/shard_map/ppermute | solution.py:36
  180.6 7.7 %shard_map.199 = (bf16[256,1536]{1,0:T(8,128)(2,1)}, bf16[256,1536]{1,0:T(8,128)(2,1)S(1)}, bf16[256,1536]{1,0:T(8,128)(2,1)S(1)}, bf16[256,1536]{1,0:T(8,128)(2...) custom-call(bf16[256,1536]{1,0:T(8,128)(2,1)S(1)} %copy-done.124, ...), custom_call_target="tpu_custom_call" | custom-call | flops 4831838208 | bytes 12582912 | tf_op jit(solution)/shard_map/pallas_call | solution.py:96
  194.2 9.8 %shard_map.200 = (bf16[256,1536]{1,0:T(8,128)(2,1)}, bf16[256,1536]{1,0:T(8,128)(2,1)S(1)}, bf16[256,1536]{1,0:T(8,128)(2,1)}, bf16[256,1536]{1,0:T(8,128)(2,1)S...) custom-call(bf16[256,1536]{1,0:T(8,128)(2,1)} %collective-permute-done.27.refs_0_.refs_2_, ...), custom_call_target="tpu_custom_call" | custom-call | flops 4831838208 | bytes 12582912 | tf_op jit(solution)/shard_map/pallas_call | solution.py:96
  207.3 4.5 collective-permute-done.39.refs_3_.refs_7_
  211.8 8.7 %shard_map.201 = (bf16[256,1536]{1,0:T(8,128)(2,1)S(1)}, bf16[256,1536]{1,0:T(8,128)(2,1)S(1)}, bf16[256,1536]{1,0:T(8,128)(2,1)S(1)}, bf16[256,1536]{1,0:T(8,12...) custom-call(bf16[256,1536]{1,0:T(8,128)(2,1)} %collective-permute-done.33.refs_0_.refs_8_, ...), custom_call_target="tpu_custom_call" | custom-call | flops 4831838208 | bytes 12582912 | tf_op jit(solution)/shard_map/pallas_call | solution.py:96
  225.0 8.2 %shard_map.202 = (bf16[256,1536]{1,0:T(8,128)(2,1)S(1)}, bf16[256,1536]{1,0:T(8,128)(2,1)S(1)}, bf16[256,1536]{1,0:T(8,128)(2,1)S(1)}, bf16[256,1536]{1,0:T(8,12...) custom-call(bf16[128,1536]{1,0:T(8,128)(2,1)S(1)} %collective-permute-done.38.refs_0_.refs_4_, ...), custom_call_target="tpu_custom_call" | custom-call | flops 4831838208 | bytes 12582912 | tf_op jit(solution)/shard_map/pallas_call | solution.py:96
  237.6 9.5 %shard_map.213 = bf16[1536,1024]{1,0:T(8,128)(2,1)S(1)} custom-call(bf16[256,1536]{1,0:T(8,128)(2,1)S(1)} %copy-done.125, bf16[256,1536]{1,0:T(8,128)(2,1)S(1)} %copy-done.122, bf16[256,1536]{1,0:T(8,128)(2,1)} %collective-permute-done.27.refs_0_.refs_2_, bf16[256,1536]{1,0:T(8,128)(2,1)} %collective-permute-done.26.refs_1_.refs_3_, ...), custom_call_target="tpu_custom_call" | custom-call | flops 6442450944 | bytes 9437184 | tf_op jit(solution)/shard_map/pallas_call | solution.py:389
  256.0 9.4 %collective-permute-done.48 = bf16[128,1536]{1,0:T(8,128)(2,1)S(1)} collective-permute-done((bf16[128,1536]{1,0:T(8,128)(2,1)S(1)}, bf16[128,1536]{1,0:T(8,128)(2,1)S(1)}, u32[]{:S(2)}, u32[]{:S(2)}) %collective-permute-start.48) | collective-permute-done | bytes 393248 | tf_op jit(solution)/shard_map/ppermute | solution.py:36
  270.1 7.6 %collective-permute-done.31.refs_2_ = bf16[128,1536]{1,0:T(8,128)(2,1)S(1)} collective-permute-done((bf16[128,1536]{1,0:T(8,128)(2,1)S(1)}, bf16[128,1536]{1,0:T(8,128)(2,1)S(1)}, u32[]{:S(2)}, u32[]{:S(2)}) %collective-permute-start.31) | collective-permute-done | bytes 393248 | tf_op jit(solution)/shard_map/ppermute | solution.py:36
  278.9 5.9 %collective-permute-done.49.refs_4_ = bf16[128,1536]{1,0:T(8,128)(2,1)S(1)} collective-permute-done((bf16[128,1536]{1,0:T(8,128)(2,1)S(1)}, bf16[128,1536]{1,0:T(8,128)(2,1)S(1)}, u32[]{:S(2)}, u32[]{:S(2)}) %collective-permute-start.49) | collective-permute-done | bytes 393248 | tf_op jit(solution)/shard_map/ppermute | solution.py:36
  290.6 16.0 %collective-permute-done.52.refs_1_.refs_7_ = bf16[256,1536]{1,0:T(8,128)(2,1)S(1)} collective-permute-done((bf16[256,1536]{1,0:T(8,128)(2,1)S(1)}, bf16[256,1536]{1,0:T(8,128)(2,1)S(1)}, u32[]{:S(2)}, u32[]{:S(2)}) %collective-permute-start.52) | collective-permute-done | bytes 786464 | tf_op jit(solution)/shard_map/ppermute | solution.py:36
  309.6 9.3 %collective-permute-done.55.refs_2_.refs_10_ = bf16[128,1536]{1,0:T(8,128)(2,1)S(1)} collective-permute-done((bf16[128,1536]{1,0:T(8,128)(2,1)S(1)}, bf16[128,1536]{1,0:T(8,128)(2,1)S(1)}, u32[]{:S(2)}, u32[]{:S(2)}) %collective-permute-start.55) | collective-permute-done | bytes 393248 | tf_op jit(solution)/shard_map/ppermute | solution.py:36
  319.9 6.9 %shard_map.205 = (bf16[256,1536]{1,0:T(8,128)(2,1)}, bf16[256,1536]{1,0:T(8,128)(2,1)S(1)}, bf16[512,512]{1,0:T(8,128)(2,1)S(1)}) custom-call(bf16[256,1536]{1,0:T(8,128)(2,1)S(1)} %collective-permute-done.51.refs_0_.refs_4_, bf16[256,1536]{1,0:T(8,128)(2,1)S(1)} %get-tuple-element.117.refs_1_.refs_5_, bf16[512,512]{1,0:T(8,128)(2,1)S(1)} %copy-done.160, ...), custom_call_target="tpu_custom_call" | custom-call | flops 1442840576 | bytes 6717440 | tf_op jit(solution)/shard_map/pallas_call | solution.py:96
  327.7 5.9 %shard_map.206 = (bf16[256,1536]{1,0:T(8,128)(2,1)S(1)}, bf16[256,1536]{1,0:T(8,128)(2,1)S(1)}, bf16[512,512]{1,0:T(8,128)(2,1)S(1)}) custom-call(bf16[256,1536]{1,0:T(8,128)(2,1)S(1)} %collective-permute-done.53.refs_0_.refs_6_, bf16[256,1536]{1,0:T(8,128)(2,1)S(1)} %collective-permute-done.52.refs_1_.refs_7_, bf16[512,512]{1,0:T(8,128)(2,1)S(1)} %copy-done.156, ...), custom_call_target="tpu_custom_call" | custom-call | flops 1442840576 | bytes 6717440 | tf_op jit(solution)/shard_map/pallas_call | solution.py:96
  335.5 5.9 %shard_map.207 = (bf16[256,1536]{1,0:T(8,128)(2,1)S(1)}, bf16[256,1536]{1,0:T(8,128)(2,1)S(1)}, bf16[512,512]{1,0:T(8,128)(2,1)S(1)}) custom-call(bf16[256,1536]{1,0:T(8,128)(2,1)S(1)} %collective-permute-done.59.refs_0_.refs_12_, bf16[256,1536]{1,0:T(8,128)(2,1)S(1)} %collective-permute-done.54.refs_1_.refs_13_, bf16[512,512]{1,0:T(8,128)(2,1)S(1)} %copy-done.158, ...), custom_call_target="tpu_custom_call" | custom-call | flops 1442840576 | bytes 6717440 | tf_op jit(solution)/shard_map/pallas_call | solution.py:96
  343.4 6.8 %shard_map.208 = (bf16[256,1536]{1,0:T(8,128)(2,1)}, bf16[256,1536]{1,0:T(8,128)(2,1)S(1)}, bf16[512,512]{1,0:T(8,128)(2,1)S(1)}) custom-call(bf16[128,1536]{1,0:T(8,128)(2,1)S(1)} %collective-permute-done.56.refs_0_.refs_8_, bf16[128,1536]{1,0:T(8,128)(2,1)S(1)} %collective-permute-done.58.refs_1_.refs_9_, ...), custom_call_target="tpu_custom_call" | custom-call | flops 1442840576 | bytes 6717440 | tf_op jit(solution)/shard_map/pallas_call | solution.py:96
  351.0 6.4 %shard_map.210 = bf16[1536,384]{1,0:T(8,128)(2,1)S(1)} custom-call(bf16[512,1536]{1,0:T(8,128)(2,1)S(1)} %copy-done.152, bf16[512,1536]{1,0:T(8,128)(2,1)S(1)} %copy-done.148, bf16[512,1536]{1,0:T(8,128)(2,1)S(1)} %copy-done.146, bf16[512,1536]{1,0:T(8,128)(2,1)S(1)} %copy-done.150, bf16[512,512]{1,0:T(8,128)(2,1)S(1)} %get-tuple-element.150.refs_4_, ...), custom_call_target="tpu_custom_call" | custom-call | flops 3221225472 | bytes 9437184 | tf_op jit(solution)/shard_map/pallas_call | solution.py:389
  368.6 7.1 %shard_map.211 = bf16[512,1536]{1,0:T(8,128)(2,1)S(1)} custom-call(bf16[512,512]{1,0:T(8,128)(2,1)S(1)} %copy-done.162, bf16[512,512]{1,0:T(8,128)(2,1)S(1)} %copy-done.164, bf16[512,512]{1,0:T(8,128)(2,1)S(1)} %copy-done.168, bf16[512,512]{1,0:T(8,128)(2,1)S(1)} %copy-done.166, bf16[256,1536]{1,0:T(8,128)(2,1)S(1)} %copy-done.112, ...), custom_call_target="tpu_custom_call" | custom-call | flops 3221225472 | bytes 9437184 | tf_op jit(solution)/shard_map/pallas_call | solution.py:389
  375.7 4.0 shard_map.212
  387.4 8.2 %collective-permute-done.67 = bf16[128,1536]{1,0:T(8,128)(2,1)S(1)} collective-permute-done((bf16[128,1536]{1,0:T(8,128)(2,1)S(1)}, bf16[128,1536]{1,0:T(8,128)(2,1)S(1)}, u32[]{:S(2)}, u32[]{:S(2)}) %collective-permute-start.67) | collective-permute-done | bytes 393248 | tf_op jit(solution)/shard_map/ppermute | solution.py:36
  397.5 8.6 %collective-permute-done.65 = bf16[128,1536]{1,0:T(8,128)(2,1)S(1)} collective-permute-done((bf16[128,1536]{1,0:T(8,128)(2,1)S(1)}, bf16[128,1536]{1,0:T(8,128)(2,1)S(1)}, u32[]{:S(2)}, u32[]{:S(2)}) %collective-permute-start.65) | collective-permute-done | bytes 393248 | tf_op jit(solution)/shard_map/ppermute | solution.py:36
  409.2 6.7 %collective-permute-done.77 = bf16[128,1536]{1,0:T(8,128)(2,1)S(1)} collective-permute-done((bf16[128,1536]{1,0:T(8,128)(2,1)S(1)}, bf16[128,1536]{1,0:T(8,128)(2,1)S(1)}, u32[]{:S(2)}, u32[]{:S(2)}) %collective-permute-start.77) | collective-permute-done | bytes 393248 | tf_op jit(solution)/shard_map/ppermute | solution.py:36
  423.1 4.8 collective-permute-done.62.refs_2_
  431.9 4.6 collective-permute-done.68.refs_4_
  439.6 5.2 collective-permute-done.72.refs_2_
  448.1 5.2 collective-permute-done.78.refs_4_
  454.0 20.2 %collective-permute-done.81.refs_2_ = bf16[384,384]{1,0:T(8,128)(2,1)S(1)} collective-permute-done((bf16[384,384]{1,0:T(8,128)(2,1)}, bf16[384,384]{1,0:T(8,128)(2,1)S(1)}, u32[]{:S(2)}, u32[]{:S(2)}) %collective-permute-start.81) | collective-permute-done | bytes 294944 | tf_op jit(solution)/shard_map/ppermute | solution.py:36
  486.8 3.2 collective-permute-start.105
  491.6 8.8 %collective-permute-start.101 = (bf16[384,1024]{1,0:T(8,128)(2,1)S(1)}, bf16[384,1024]{1,0:T(8,128)(2,1)S(1)}, u32[]{:S(2)}, u32[]{:S(2)}) collective-permute-start(bf16[384,1024]{1,0:T(8,128)(2,1)S(1)} %collective-permute-done.100.refs_2_), channel_id=1, source_target_pairs={{0,4},{4,0},{8,12},{12,8},{16,20},{20,16},{24,28},{28,24},{1,5},{5... | collective-permute-start | bytes 2359304 | tf_op jit(solution)/shard_map/ppermute | solution.py:36
  502.8 12.9 %collective-permute-done.91.refs_2_ = bf16[176,1536]{1,0:T(8,128)(2,1)} collective-permute-done((bf16[176,1536]{1,0:T(8,128)(2,1)}, bf16[176,1536]{1,0:T(8,128)(2,1)}, u32[]{:S(2)}, u32[]{:S(2)}) %collective-permute-start.91) | collective-permute-done | bytes 540704 | tf_op jit(solution)/shard_map/ppermute | solution.py:36
  526.6 2.6 shard_map.204
  529.3 3.8 shard_map.209
  533.2 4.9 spread_attn.1
  553.0 16.0 %spread_wide.1 = (f32[384,4096]{1,0:T(8,128)}, f32[384,4096]{1,0:T(8,128)}, f32[384,128]{1,0:T(8,128)S(1)}) custom-call(s32[1]{0:T(128)} %bitcast.9.at_ref, bf16[384,1024]{1,0:T(8,128)(2,1)S(1)} %copy-done.21, bf16[384,1024]{1,0:T(8,128)(2,1)S(1)} %copy-done.27, bf16[384,1024]{1,0:T(8,128)(2,1)S(1)} %copy-done.10, bf16[384,1024]{1,0:T(8,128)(2,1)S(1)} %copy-done.29, ...), custom_call_target="tpu_custom_call" | custom-call | bytes 25165824 | tf_op jit(solution)/shard_map/spread_wide/pallas_call | solution.py:473
  571.4 7.0 %spread_rows.1 = (f32[1024,1536]{1,0:T(8,128)}, f32[384,1536]{1,0:T(8,128)}) custom-call(s32[1]{0:T(128)} %bitcast.9.at_ref, bf16[176,1536]{1,0:T(8,128)(2,1)} %pad_maximum_fusion.2.refs_0_, bf16[176,1536]{1,0:T(8,128)(2,1)} %collective-permute-done.90.refs_1_, bf16[176,1536]{1,0:T(8,128)(2,1)} %collective-permute-done.91.refs_2_, ...), custom_call_target="tpu_custom_call" | custom-call | bytes 12976128 | tf_op jit(solution)/shard_map/spread_rows/pallas_call | solution.py:514
  (627 shorter events, 218.5 us)
Async XLA Ops:
  7.2 58.1 %all-gather.4.cloned.1.call-start = ((), (), s32[]{:S(2)}) async-start(), calls=%async_computation.3 | async-start | bytes 1536000 | tf_op jit(solution)/shard_map/all_gather | solution.py:602
  12.0 160.8 %all-gather.8.cloned.1.call-start = ((), (), s32[]{:S(2)}) async-start(), calls=%async_computation.5 | async-start | bytes 1966080 | tf_op jit(solution)/shard_map/all_gather | solution.py:602
  12.9 159.9 %all-gather.6.cloned.1.call-start = ((), (), s32[]{:S(2)}) async-start(), calls=%async_computation.4 | async-start | bytes 3932160 | tf_op jit(solution)/shard_map/all_gather | solution.py:602
  14.5 39.0 %collective-permute-start.4 = (bf16[48,1536]{1,0:T(8,128)(2,1)}, bf16[48,1536]{1,0:T(8,128)(2,1)S(1)}, u32[]{:S(2)}, u32[]{:S(2)}) collective-permute-start(bf16[48,1536]{1,0:T(8,128)(2,1)} %constant_dynamic-slice_fusion.1), channel_id=1, source_target_pairs={{0,3},{1,11},{2,19},{3,27},{4,0},{5,8},{6,16},{7,24},{8,1},{9,9},{... | collective-permute-start | bytes 442376 | tf_op jit(solution)/shard_map/ppermute | solution.py:657
  21.5 33.9 %collective-permute-start.3 = (bf16[48,1536]{1,0:T(8,128)(2,1)}, bf16[48,1536]{1,0:T(8,128)(2,1)}, u32[]{:S(2)}, u32[]{:S(2)}) collective-permute-start(bf16[48,1536]{1,0:T(8,128)(2,1)} %constant_dynamic-slice_fusion.1), channel_id=1, source_target_pairs={{0,2},{1,10},{2,18},{3,26},{4,3},{5,11},{6,19},{7,27},{8,0},{9,8},... | collective-permute-start | bytes 442376 | tf_op jit(solution)/shard_map/ppermute | solution.py:657
  23.1 32.4 %collective-permute-start.2 = (bf16[48,1536]{1,0:T(8,128)(2,1)}, bf16[48,1536]{1,0:T(8,128)(2,1)}, u32[]{:S(2)}, u32[]{:S(2)}) collective-permute-start(bf16[48,1536]{1,0:T(8,128)(2,1)} %constant_dynamic-slice_fusion.1), channel_id=1, source_target_pairs={{0,1},{1,9},{2,17},{3,25},{4,2},{5,10},{6,18},{7,26},{8,3},{9,11},... | collective-permute-start | bytes 442376 | tf_op jit(solution)/shard_map/ppermute | solution.py:657
  25.3 22.0 %collective-permute-start.10 = (bf16[256,1536]{1,0:T(8,128)(2,1)}, bf16[256,1536]{1,0:T(8,128)(2,1)S(1)}, u32[]{:S(2)}, u32[]{:S(2)}) collective-permute-start(bf16[256,1536]{1,0:T(8,128)(2,1)} %refs_6_.3), channel_id=1, source_target_pairs={{0,16},{4,20},{8,24},{12,28},{16,0},{20,4},{24,8},{28,12},{1,17},{... | collective-permute-start | bytes 2359304 | tf_op jit(solution)/shard_map/ppermute | solution.py:36
  27.5 21.7 %collective-permute-start.6 = (bf16[256,1536]{1,0:T(8,128)(2,1)}, bf16[256,1536]{1,0:T(8,128)(2,1)}, u32[]{:S(2)}, u32[]{:S(2)}) collective-permute-start(bf16[256,1536]{1,0:T(8,128)(2,1)} %refs_6_.3), channel_id=1, source_target_pairs={{0,8},{4,12},{8,0},{12,4},{16,24},{20,28},{24,16},{28,20},{1,9},{5... | collective-permute-start | bytes 2359304 | tf_op jit(solution)/shard_map/ppermute | solution.py:36
  37.0 393.6 %reduce-scatter.8.cloned.1.call-start = ((), (), s32[]{:S(2)}) async-start(), calls=%async_computation.8 | async-start | bytes 3932160 | tf_op jit(solution)/shard_map/reduce_scatter | solution.py:606
  58.0 22.9 %collective-permute-start.7 = (bf16[256,1536]{1,0:T(8,128)(2,1)}, bf16[256,1536]{1,0:T(8,128)(2,1)}, u32[]{:S(2)}, u32[]{:S(2)}) collective-permute-start(bf16[256,1536]{1,0:T(8,128)(2,1)} %collective-permute-done.6.refs_1_), channel_id=1, source_target_pairs={{0,4},{4,0},{8,12},{12,8},{16,20},{20,16},{24,28},{28,24},{1,5},{5... | collective-permute-start | bytes 2359304 | tf_op jit(solution)/shard_map/ppermute | solution.py:36
  94.0 41.9 %collective-permute-start.34 = (bf16[256,1536]{1,0:T(8,128)(2,1)S(1)}, bf16[256,1536]{1,0:T(8,128)(2,1)}, u32[]{:S(2)}, u32[]{:S(2)}) collective-permute-start(bf16[256,1536]{1,0:T(8,128)(2,1)S(1)} %copy-done.48), channel_id=1, source_target_pairs={{0,16},{4,20},{8,24},{12,28},{16,0},{20,4},{24,8},{28,12},{1,17},{... | collective-permute-start | bytes 2359304 | tf_op jit(solution)/shard_map/ppermute | solution.py:36
  119.7 25.4 %collective-permute-start.28 = (bf16[256,1536]{1,0:T(8,128)(2,1)S(1)}, bf16[256,1536]{1,0:T(8,128)(2,1)}, u32[]{:S(2)}, u32[]{:S(2)}) collective-permute-start(bf16[256,1536]{1,0:T(8,128)(2,1)S(1)} %copy-done.48), channel_id=1, source_target_pairs={{0,8},{4,12},{8,0},{12,4},{16,24},{20,28},{24,16},{28,20},{1,9},{5... | collective-permute-start | bytes 2359304 | tf_op jit(solution)/shard_map/ppermute | solution.py:36
  132.9 28.7 %collective-permute-start.26 = (bf16[256,1536]{1,0:T(8,128)(2,1)S(1)}, bf16[256,1536]{1,0:T(8,128)(2,1)}, u32[]{:S(2)}, u32[]{:S(2)}) collective-permute-start(bf16[256,1536]{1,0:T(8,128)(2,1)S(1)} %get-tuple-element.102.refs_1_), channel_id=1, source_target_pairs={{0,8},{4,12},{8,0},{12,4},{16,24},{20,28},{24,16},{28,20},{1,9},{5... | collective-permute-start | bytes 2359304 | tf_op jit(solution)/shard_map/ppermute | solution.py:36
  134.8 32.2 %collective-permute-start.32 = (bf16[256,1536]{1,0:T(8,128)(2,1)S(1)}, bf16[256,1536]{1,0:T(8,128)(2,1)}, u32[]{:S(2)}, u32[]{:S(2)}) collective-permute-start(bf16[256,1536]{1,0:T(8,128)(2,1)S(1)} %get-tuple-element.102.refs_1_), channel_id=1, source_target_pairs={{0,16},{4,20},{8,24},{12,28},{16,0},{20,4},{24,8},{28,12},{1,17},{... | collective-permute-start | bytes 2359304 | tf_op jit(solution)/shard_map/ppermute | solution.py:36
  135.9 34.6 %collective-permute-start.24 = (bf16[256,1536]{1,0:T(8,128)(2,1)S(1)}, bf16[256,1536]{1,0:T(8,128)(2,1)S(1)}, u32[]{:S(2)}, u32[]{:S(2)}) collective-permute-start(bf16[256,1536]{1,0:T(8,128)(2,1)S(1)} %copy-done.48), channel_id=1, source_target_pairs={{0,4},{4,0},{8,12},{12,8},{16,20},{20,16},{24,28},{28,24},{1,5},{5... | collective-permute-start | bytes 2359304 | tf_op jit(solution)/shard_map/ppermute | solution.py:36
  135.9 35.7 %collective-permute-start.23 = (bf16[256,1536]{1,0:T(8,128)(2,1)S(1)}, bf16[256,1536]{1,0:T(8,128)(2,1)S(1)}, u32[]{:S(2)}, u32[]{:S(2)}) collective-permute-start(bf16[256,1536]{1,0:T(8,128)(2,1)S(1)} %get-tuple-element.102.refs_1_), channel_id=1, source_target_pairs={{0,4},{4,0},{8,12},{12,8},{16,20},{20,16},{24,28},{28,24},{1,5},{5... | collective-permute-start | bytes 2359304 | tf_op jit(solution)/shard_map/ppermute | solution.py:36
  145.1 47.8 %collective-permute-start.29 = (bf16[256,1536]{1,0:T(8,128)(2,1)}, bf16[256,1536]{1,0:T(8,128)(2,1)}, u32[]{:S(2)}, u32[]{:S(2)}) collective-permute-start(bf16[256,1536]{1,0:T(8,128)(2,1)} %collective-permute-done.28.refs_3_.refs_7_), channel_id=1, source_target_pairs={{0,4},{4,0},{8,12},{12,8},{16,20},{20,16},{24,28},{28,24},{1,5},{5... | collective-permute-start | bytes 2359304 | tf_op jit(solution)/shard_map/ppermute | solution.py:36
  161.6 32.0 %collective-permute-start.27 = (bf16[256,1536]{1,0:T(8,128)(2,1)}, bf16[256,1536]{1,0:T(8,128)(2,1)}, u32[]{:S(2)}, u32[]{:S(2)}) collective-permute-start(bf16[256,1536]{1,0:T(8,128)(2,1)} %collective-permute-done.26.refs_1_.refs_3_), channel_id=1, source_target_pairs={{0,4},{4,0},{8,12},{12,8},{16,20},{20,16},{24,28},{28,24},{1,5},{5... | collective-permute-start | bytes 2359304 | tf_op jit(solution)/shard_map/ppermute | solution.py:36
  166.9 24.9 %collective-permute-start.41 = (bf16[128,1536]{1,0:T(8,128)(2,1)}, bf16[128,1536]{1,0:T(8,128)(2,1)}, u32[]{:S(2)}, u32[]{:S(2)}) collective-permute-start(bf16[128,1536]{1,0:T(8,128)(2,1)} %slice.292), channel_id=1, source_target_pairs={{0,8},{4,12},{8,0},{12,4},{16,24},{20,28},{24,16},{28,20},{1,9},{5... | collective-permute-start | bytes 1179656 | tf_op jit(solution)/shard_map/ppermute | solution.py:36
  171.4 35.3 %collective-permute-start.35 = (bf16[256,1536]{1,0:T(8,128)(2,1)}, bf16[256,1536]{1,0:T(8,128)(2,1)}, u32[]{:S(2)}, u32[]{:S(2)}) collective-permute-start(bf16[256,1536]{1,0:T(8,128)(2,1)} %collective-permute-done.34.refs_3_.refs_13_), channel_id=1, source_target_pairs={{0,4},{4,0},{8,12},{12,8},{16,20},{20,16},{24,28},{28,24},{1,5},{5... | collective-permute-start | bytes 2359304 | tf_op jit(solution)/shard_map/ppermute | solution.py:36
  172.5 39.3 %collective-permute-start.33 = (bf16[256,1536]{1,0:T(8,128)(2,1)}, bf16[256,1536]{1,0:T(8,128)(2,1)}, u32[]{:S(2)}, u32[]{:S(2)}) collective-permute-start(bf16[256,1536]{1,0:T(8,128)(2,1)} %collective-permute-done.32.refs_1_.refs_9_), channel_id=1, source_target_pairs={{0,4},{4,0},{8,12},{12,8},{16,20},{20,16},{24,28},{28,24},{1,5},{5... | collective-permute-start | bytes 2359304 | tf_op jit(solution)/shard_map/ppermute | solution.py:36
  248.8 196.7 %reduce-scatter.4.cloned.1.call-start = ((), (), s32[]{:S(2)}) async-start(), calls=%async_computation.6 | async-start | bytes 1474560 | tf_op jit(solution)/shard_map/reduce_scatter | solution.py:606
  290.6 29.2 %collective-permute-start.51 = (bf16[256,1536]{1,0:T(8,128)(2,1)S(1)}, bf16[256,1536]{1,0:T(8,128)(2,1)S(1)}, u32[]{:S(2)}, u32[]{:S(2)}) collective-permute-start(bf16[256,1536]{1,0:T(8,128)(2,1)S(1)} %get-tuple-element.117.refs_1_.refs_5_), channel_id=1, source_target_pairs={{0,4},{4,0},{8,12},{12,8},{16,20},{20,16},{24,28},{28,24},{1,5},{5... | collective-permute-start | bytes 2359304 | tf_op jit(solution)/shard_map/ppermute | solution.py:36
  306.6 21.1 %collective-permute-start.53 = (bf16[256,1536]{1,0:T(8,128)(2,1)S(1)}, bf16[256,1536]{1,0:T(8,128)(2,1)S(1)}, u32[]{:S(2)}, u32[]{:S(2)}) collective-permute-start(bf16[256,1536]{1,0:T(8,128)(2,1)S(1)} %collective-permute-done.52.refs_1_.refs_7_), channel_id=1, source_target_pairs={{0,4},{4,0},{8,12},{12,8},{16,20},{20,16},{24,28},{28,24},{1,5},{5... | collective-permute-start | bytes 2359304 | tf_op jit(solution)/shard_map/ppermute | solution.py:36
  307.2 28.3 %collective-permute-start.59 = (bf16[256,1536]{1,0:T(8,128)(2,1)S(1)}, bf16[256,1536]{1,0:T(8,128)(2,1)S(1)}, u32[]{:S(2)}, u32[]{:S(2)}) collective-permute-start(bf16[256,1536]{1,0:T(8,128)(2,1)S(1)} %collective-permute-done.54.refs_1_.refs_13_), channel_id=1, source_target_pairs={{0,4},{4,0},{8,12},{12,8},{16,20},{20,16},{24,28},{28,24},{1,5},{5... | collective-permute-start | bytes 2359304 | tf_op jit(solution)/shard_map/ppermute | solution.py:36
  318.9 24.4 %collective-permute-start.56 = (bf16[128,1536]{1,0:T(8,128)(2,1)S(1)}, bf16[128,1536]{1,0:T(8,128)(2,1)S(1)}, u32[]{:S(2)}, u32[]{:S(2)}) collective-permute-start(bf16[128,1536]{1,0:T(8,128)(2,1)S(1)} %collective-permute-done.55.refs_2_.refs_10_), channel_id=1, source_target_pairs={{0,4},{4,0},{8,12},{12,8},{16,20},{20,16},{24,28},{28,24},{1,5},{5... | collective-permute-start | bytes 1179656 | tf_op jit(solution)/shard_map/ppermute | solution.py:36
  319.8 23.5 %collective-permute-start.58 = (bf16[128,1536]{1,0:T(8,128)(2,1)S(1)}, bf16[128,1536]{1,0:T(8,128)(2,1)S(1)}, u32[]{:S(2)}, u32[]{:S(2)}) collective-permute-start(bf16[128,1536]{1,0:T(8,128)(2,1)S(1)} %collective-permute-done.57.refs_3_.refs_11_), channel_id=1, source_target_pairs={{0,4},{4,0},{8,12},{12,8},{16,20},{20,16},{24,28},{28,24},{1,5},{5... | collective-permute-start | bytes 1179656 | tf_op jit(solution)/shard_map/ppermute | solution.py:36
  358.4 126.0 %reduce-scatter.6.cloned.1.call-start = ((), (), s32[]{:S(2)}) async-start(), calls=%async_computation.7 | async-start | bytes 2703360 | tf_op jit(solution)/shard_map/reduce_scatter | solution.py:606
  358.5 23.9 %collective-permute-start.64 = (bf16[256,1536]{1,0:T(8,128)(2,1)}, bf16[256,1536]{1,0:T(8,128)(2,1)}, u32[]{:S(2)}, u32[]{:S(2)}) collective-permute-start(bf16[256,1536]{1,0:T(8,128)(2,1)} %copy-done.114), channel_id=1, source_target_pairs={{0,4},{4,0},{8,12},{12,8},{16,20},{20,16},{24,28},{28,24},{1,5},{5... | collective-permute-start | bytes 2359304 | tf_op jit(solution)/shard_map/ppermute | solution.py:36
  381.4 36.4 %collective-permute-start.70 = (bf16[256,1536]{1,0:T(8,128)(2,1)}, bf16[256,1536]{1,0:T(8,128)(2,1)S(1)}, u32[]{:S(2)}, u32[]{:S(2)}) collective-permute-start(bf16[256,1536]{1,0:T(8,128)(2,1)} %get-tuple-element.135), channel_id=1, source_target_pairs={{0,4},{4,0},{8,12},{12,8},{16,20},{20,16},{24,28},{28,24},{1,5},{5... | collective-permute-start | bytes 2359304 | tf_op jit(solution)/shard_map/ppermute | solution.py:36
  381.9 37.2 %collective-permute-start.60 = (bf16[256,1536]{1,0:T(8,128)(2,1)}, bf16[256,1536]{1,0:T(8,128)(2,1)S(1)}, u32[]{:S(2)}, u32[]{:S(2)}) collective-permute-start(bf16[256,1536]{1,0:T(8,128)(2,1)} %get-tuple-element.120), channel_id=1, source_target_pairs={{0,4},{4,0},{8,12},{12,8},{16,20},{20,16},{24,28},{28,24},{1,5},{5... | collective-permute-start | bytes 2359304 | tf_op jit(solution)/shard_map/ppermute | solution.py:36
  387.3 20.6 %collective-permute-start.71 = (bf16[256,1536]{1,0:T(8,128)(2,1)S(1)}, bf16[256,1536]{1,0:T(8,128)(2,1)S(1)}, u32[]{:S(2)}, u32[]{:S(2)}) collective-permute-start(bf16[256,1536]{1,0:T(8,128)(2,1)S(1)} %copy-done.119), channel_id=1, source_target_pairs={{0,4},{4,0},{8,12},{12,8},{16,20},{20,16},{24,28},{28,24},{1,5},{5... | collective-permute-start | bytes 2359304 | tf_op jit(solution)/shard_map/ppermute | solution.py:36
  397.5 22.3 %collective-permute-start.73 = (bf16[256,1536]{1,0:T(8,128)(2,1)S(1)}, bf16[256,1536]{1,0:T(8,128)(2,1)S(1)}, u32[]{:S(2)}, u32[]{:S(2)}) collective-permute-start(bf16[256,1536]{1,0:T(8,128)(2,1)S(1)} %copy-done.116), channel_id=1, source_target_pairs={{0,4},{4,0},{8,12},{12,8},{16,20},{20,16},{24,28},{28,24},{1,5},{5... | collective-permute-start | bytes 2359304 | tf_op jit(solution)/shard_map/ppermute | solution.py:36
  419.8 18.6 %collective-permute-start.69 = (bf16[128,1536]{1,0:T(8,128)(2,1)}, bf16[128,1536]{1,0:T(8,128)(2,1)}, u32[]{:S(2)}, u32[]{:S(2)}) collective-permute-start(bf16[128,1536]{1,0:T(8,128)(2,1)} %get-tuple-element.181), channel_id=1, source_target_pairs={{0,16},{4,20},{8,24},{12,28},{16,0},{20,4},{24,8},{28,12},{1,17},{... | collective-permute-start | bytes 1179656 | tf_op jit(solution)/shard_map/ppermute | solution.py:36
  421.1 23.6 %collective-permute-start.72 = (bf16[128,1536]{1,0:T(8,128)(2,1)}, bf16[128,1536]{1,0:T(8,128)(2,1)S(1)}, u32[]{:S(2)}, u32[]{:S(2)}) collective-permute-start(bf16[128,1536]{1,0:T(8,128)(2,1)} %get-tuple-element.178), channel_id=1, source_target_pairs={{0,8},{4,12},{8,0},{12,4},{16,24},{20,28},{24,16},{28,20},{1,9},{5... | collective-permute-start | bytes 1179656 | tf_op jit(solution)/shard_map/ppermute | solution.py:36
  430.6 49.1 %collective-permute-start.102 = (bf16[384,1024]{1,0:T(8,128)(2,1)}, bf16[384,1024]{1,0:T(8,128)(2,1)S(1)}, u32[]{:S(2)}, u32[]{:S(2)}) collective-permute-start(bf16[384,1024]{1,0:T(8,128)(2,1)} %reduce-scatter.8.cloned.1.call-done.refs_0_), channel_id=1, source_target_pairs={{0,16},{4,20},{8,24},{12,28},{16,0},{20,4},{24,8},{28,12},{1,17},{... | collective-permute-start | bytes 2359304 | tf_op jit(solution)/shard_map/ppermute | solution.py:36
  438.4 47.7 %collective-permute-start.100 = (bf16[384,1024]{1,0:T(8,128)(2,1)}, bf16[384,1024]{1,0:T(8,128)(2,1)S(1)}, u32[]{:S(2)}, u32[]{:S(2)}) collective-permute-start(bf16[384,1024]{1,0:T(8,128)(2,1)} %reduce-scatter.8.cloned.1.call-done.refs_0_), channel_id=1, source_target_pairs={{0,8},{4,12},{8,0},{12,4},{16,24},{20,28},{24,16},{28,20},{1,9},{5... | collective-permute-start | bytes 2359304 | tf_op jit(solution)/shard_map/ppermute | solution.py:36
  445.5 28.6 %collective-permute-start.81 = (bf16[384,384]{1,0:T(8,128)(2,1)}, bf16[384,384]{1,0:T(8,128)(2,1)S(1)}, u32[]{:S(2)}, u32[]{:S(2)}) collective-permute-start(bf16[384,384]{1,0:T(8,128)(2,1)} %reduce-scatter.4.cloned.1.call-done.refs_0_), channel_id=1, source_target_pairs={{0,8},{4,12},{8,0},{12,4},{16,24},{20,28},{24,16},{28,20},{1,9},{5... | collective-permute-start | bytes 884744 | tf_op jit(solution)/shard_map/ppermute | solution.py:36
  446.8 29.2 %collective-permute-start.79 = (bf16[128,1536]{1,0:T(8,128)(2,1)}, bf16[128,1536]{1,0:T(8,128)(2,1)S(1)}, u32[]{:S(2)}, u32[]{:S(2)}) collective-permute-start(bf16[128,1536]{1,0:T(8,128)(2,1)} %get-tuple-element.175), channel_id=1, source_target_pairs={{0,16},{4,20},{8,24},{12,28},{16,0},{20,4},{24,8},{28,12},{1,17},{... | collective-permute-start | bytes 1179656 | tf_op jit(solution)/shard_map/ppermute | solution.py:36
  453.3 21.8 %collective-permute-start.83 = (bf16[384,384]{1,0:T(8,128)(2,1)}, bf16[384,384]{1,0:T(8,128)(2,1)}, u32[]{:S(2)}, u32[]{:S(2)}) collective-permute-start(bf16[384,384]{1,0:T(8,128)(2,1)} %reduce-scatter.4.cloned.1.call-done.refs_0_), channel_id=1, source_target_pairs={{0,16},{4,20},{8,24},{12,28},{16,0},{20,4},{24,8},{28,12},{1,17},{... | collective-permute-start | bytes 884744 | tf_op jit(solution)/shard_map/ppermute | solution.py:36
  491.1 28.5 %collective-permute-start.99 = (bf16[384,1024]{1,0:T(8,128)(2,1)}, bf16[384,1024]{1,0:T(8,128)(2,1)S(1)}, u32[]{:S(2)}, u32[]{:S(2)}) collective-permute-start(bf16[384,1024]{1,0:T(8,128)(2,1)} %reduce-scatter.8.cloned.1.call-done.refs_0_), channel_id=1, source_target_pairs={{0,4},{4,0},{8,12},{12,8},{16,20},{20,16},{24,28},{28,24},{1,5},{5... | collective-permute-start | bytes 2359304 | tf_op jit(solution)/shard_map/ppermute | solution.py:36
  491.6 30.1 %collective-permute-start.101 = (bf16[384,1024]{1,0:T(8,128)(2,1)S(1)}, bf16[384,1024]{1,0:T(8,128)(2,1)S(1)}, u32[]{:S(2)}, u32[]{:S(2)}) collective-permute-start(bf16[384,1024]{1,0:T(8,128)(2,1)S(1)} %collective-permute-done.100.refs_2_), channel_id=1, source_target_pairs={{0,4},{4,0},{8,12},{12,8},{16,20},{20,16},{24,28},{28,24},{1,5},{5... | collective-permute-start | bytes 2359304 | tf_op jit(solution)/shard_map/ppermute | solution.py:36
  502.8 20.7 %collective-permute-start.103 = (bf16[384,1024]{1,0:T(8,128)(2,1)S(1)}, bf16[384,1024]{1,0:T(8,128)(2,1)S(1)}, u32[]{:S(2)}, u32[]{:S(2)}) collective-permute-start(bf16[384,1024]{1,0:T(8,128)(2,1)S(1)} %collective-permute-done.102.refs_4_), channel_id=1, source_target_pairs={{0,4},{4,0},{8,12},{12,8},{16,20},{20,16},{24,28},{28,24},{1,5},{5... | collective-permute-start | bytes 2359304 | tf_op jit(solution)/shard_map/ppermute | solution.py:36
  524.5 46.9 %collective-permute-start.90 = (bf16[176,1536]{1,0:T(8,128)(2,1)}, bf16[176,1536]{1,0:T(8,128)(2,1)}, u32[]{:S(2)}, u32[]{:S(2)}) collective-permute-start(bf16[176,1536]{1,0:T(8,128)(2,1)} %pad_maximum_fusion.2.refs_0_), channel_id=1, source_target_pairs={{0,4},{4,0},{8,12},{12,8},{16,20},{20,16},{24,28},{28,24},{1,5},{5... | collective-permute-start | bytes 1622024 | tf_op jit(solution)/shard_map/ppermute | solution.py:36
  525.2 46.2 %collective-permute-start.92 = (bf16[176,1536]{1,0:T(8,128)(2,1)}, bf16[176,1536]{1,0:T(8,128)(2,1)}, u32[]{:S(2)}, u32[]{:S(2)}) collective-permute-start(bf16[176,1536]{1,0:T(8,128)(2,1)} %collective-permute-done.91.refs_2_), channel_id=1, source_target_pairs={{0,4},{4,0},{8,12},{12,8},{16,20},{20,16},{24,28},{28,24},{1,5},{5... | collective-permute-start | bytes 1622024 | tf_op jit(solution)/shard_map/ppermute | solution.py:36
  526.5 44.9 %collective-permute-start.94 = (bf16[176,1536]{1,0:T(8,128)(2,1)}, bf16[176,1536]{1,0:T(8,128)(2,1)}, u32[]{:S(2)}, u32[]{:S(2)}) collective-permute-start(bf16[176,1536]{1,0:T(8,128)(2,1)} %collective-permute-done.93.refs_4_), channel_id=1, source_target_pairs={{0,4},{4,0},{8,12},{12,8},{16,20},{20,16},{24,28},{28,24},{1,5},{5... | collective-permute-start | bytes 1622024 | tf_op jit(solution)/shard_map/ppermute | solution.py:36
  538.2 33.2 %collective-permute-start.97 = (bf16[88,1536]{1,0:T(8,128)(2,1)}, bf16[88,1536]{1,0:T(8,128)(2,1)S(1)}, u32[]{:S(2)}, u32[]{:S(2)}) collective-permute-start(bf16[88,1536]{1,0:T(8,128)(2,1)} %collective-permute-done.95.refs_6_), channel_id=1, source_target_pairs={{0,4},{4,0},{8,12},{12,8},{16,20},{20,16},{24,28},{28,24},{1,5},{5... | collective-permute-start | bytes 811016 | tf_op jit(solution)/shard_map/ppermute | solution.py:36
  538.8 32.7 %collective-permute-start.98 = (bf16[88,1536]{1,0:T(8,128)(2,1)}, bf16[88,1536]{1,0:T(8,128)(2,1)}, u32[]{:S(2)}, u32[]{:S(2)}) collective-permute-start(bf16[88,1536]{1,0:T(8,128)(2,1)} %collective-permute-done.96.refs_7_), channel_id=1, source_target_pairs={{0,4},{4,0},{8,12},{12,8},{16,20},{20,16},{24,28},{28,24},{1,5},{5... | collective-permute-start | bytes 811016 | tf_op jit(solution)/shard_map/ppermute | solution.py:36
  (239 other events, 2254.6 us)
Sparse Core Ops, SparseCore 0:
  12.1 38.9 all-gather.3
  53.3 43.2 all-gather.7
  98.7 62.2 all-gather.5
  248.9 58.2 reduce-scatter.7
  358.5 27.1 reduce-scatter.3
  388.5 43.2 reduce-scatter.5
